TPU v7x, 32 devices: a whole 2x2x4 slice. The times are simulated.
32 devices in a mesh: fsdp: 16 (over z, y, x), tp: 2 (over core).
Axes of the slice: x: 2, y: 2, z: 4, core: 2. Of those that a mesh axis runs over, the one named last changes fastest.
Arguments:
- tokens: bfloat16 [2, 16384, 512], P(None, ('fsdp', 'tp')), may hold values from -6 to 6
- gain_attn: float32 [512], replicated, may hold values from 0.5 to 1.5
- gain_ffn: float32 [512], replicated, may hold values from 0.5 to 1.5
- w_query: bfloat16 [512, 512], P('fsdp', 'tp'), may hold values from -0.25 to 0.25
- w_key: bfloat16 [512, 512], P('fsdp', 'tp'), may hold values from -0.25 to 0.25
- w_value: bfloat16 [512, 512], P('fsdp', 'tp'), may hold values from -0.25 to 0.25
- w_out: bfloat16 [512, 512], P('tp', 'fsdp'), may hold values from -0.75 to 0.75
- w_in: bfloat16 [512, 2048], P('fsdp', 'tp'), may hold values from -0.25 to 0.25
- w_down: bfloat16 [2048, 512], P('tp', 'fsdp'), may hold values from -0.125 to 0.125
- segment_ids: int32 [2, 512], P(None, 'fsdp'), may hold values from 0 to 4, as said below
- cotangent: bfloat16 [2, 16384, 512], P(None, ('fsdp', 'tp')), may hold values from -6 to 6
Outputs:
- result: bfloat16 [2, 16384, 512], P(None, ('fsdp', 'tp'))
- grad_tokens: bfloat16 [2, 16384, 512], P(None, ('fsdp', 'tp'))
- grad_gain_attn: float32 [512], P(('fsdp', 'tp'))
- grad_gain_ffn: float32 [512], P(('fsdp', 'tp'))
- grad_query: float32 [512, 512], P('fsdp', 'tp')
- grad_key: float32 [512, 512], P('fsdp', 'tp')
- grad_value: float32 [512, 512], P('fsdp', 'tp')
- grad_out: float32 [512, 512], P('tp', 'fsdp')
- grad_in: float32 [512, 2048], P('fsdp', 'tp')
- grad_down: float32 [2048, 512], P('tp', 'fsdp')
Inputs may be any that keep to these rules, and one draw needn't show every extreme that they name: `segment_ids`: within each group of 32 blocks of a micro-batch the ids never fall, begin with a prompt of 0s over a quarter to a half of the blocks, and every id 1 to 4 names a run of one block or more.
All inputs are finite; a program needn't handle non-finite values.
Results may differ from a plain program's by a relative error of at most 0.014.
Values may be sent and summed in bfloat16 or wider, within the bound.
A program may use at most 192 MiB of HBM per device.

v0:
```python
from functools import partial
import math

import jax
import jax.numpy as jnp
from jax import lax
from jax.sharding import PartitionSpec as P

HEAD_DIM = 64
BLK = 32
ITERS = 8


highest = lax.Precision.HIGHEST
epsilon = 1e-05


def quantized_result(values):
    lowered = lax.optimization_barrier(values.astype(jnp.bfloat16)).astype(jnp.float32)
    return values + lax.stop_gradient(lowered - values)


def layer_norm(values, gain_vec):
    center = values - jnp.mean(values, axis=-1, keepdims=True)
    spread = jnp.mean(center * center, axis=-1, keepdims=True)
    return center * lax.rsqrt(spread + epsilon) * gain_vec


def block_mask(segment):
    blocks = segment.shape[0]
    rows_at = jnp.arange(blocks)[:, None]
    cols_at = jnp.arange(blocks)[None, :]
    within = (segment[:, None] == segment[None, :]) & (cols_at <= rows_at)
    prompt = (segment[None, :] == 0) & (segment[:, None] > 0)
    return within | prompt


def balanced_transport_kernel(
    query_rows, incoming_keys, incoming_values, permitted_mask, quantize_helper
):
    head_count, length, head_width = query_rows.shape
    blocks = length // BLK
    query_b = query_rows.reshape(head_count, blocks, BLK, head_width)
    keys_b = incoming_keys.reshape(head_count, blocks, BLK, head_width)
    values_b = incoming_values.reshape(head_count, blocks, BLK, head_width)
    query_mean = jnp.mean(query_b, axis=2)
    keys_mean = jnp.mean(keys_b, axis=2)
    logits = jnp.einsum("hid,hjd->hij", query_mean, keys_mean, precision=highest) * (
        BLK / math.sqrt(head_width)
    )
    logits = jnp.where(permitted_mask[None], logits, -1000000000.0)
    for sweep in range(ITERS):
        logits = logits - jax.nn.logsumexp(logits, axis=2, keepdims=True)
        logits = logits - jax.nn.logsumexp(logits, axis=1, keepdims=True)
    sorter = quantize_helper(jnp.exp(logits))
    keys_sorted = quantize_helper(jnp.einsum("hij,hjrd->hird", sorter, keys_b, precision=highest))
    values_sorted = quantize_helper(
        jnp.einsum("hij,hjrd->hird", sorter, values_b, precision=highest)
    )
    score_scale = 1.0 / math.sqrt(head_width)
    causal = jnp.arange(BLK)[:, None] >= jnp.arange(BLK)[None, :]
    local_scores = jnp.einsum("hird,hisd->hirs", query_b, keys_b, precision=highest) * score_scale
    local_scores = jnp.where(causal, local_scores, -1000000000.0)
    sorted_scores = (
        jnp.einsum("hird,hisd->hirs", query_b, keys_sorted, precision=highest) * score_scale
    )
    scores = jnp.concatenate([local_scores, sorted_scores], axis=3)
    probs = quantize_helper(jax.nn.softmax(scores, axis=3))
    blended_values = jnp.einsum("hirs,hisd->hird", probs[..., :BLK], values_b, precision=highest)
    blended_values = blended_values + jnp.einsum(
        "hirs,hisd->hird", probs[..., BLK:], values_sorted, precision=highest
    )
    return blended_values.reshape(head_count, length, head_width)


def product(left_arg, right_arg):
    return jnp.dot(left_arg, right_arg, preferred_element_type=jnp.float32)


def inner_rows(left_arg, right_arg):
    return lax.dot_general(
        left_arg, right_arg, (((0,), (0,)), ((), ())), preferred_element_type=jnp.float32
    )


def outer_cols(left_arg, right_arg):
    return lax.dot_general(
        left_arg, right_arg, (((1,), (1,)), ((), ())), preferred_element_type=jnp.float32
    )


def row_slice(values, first_row, row_count):
    return lax.dynamic_slice_in_dim(values, first_row, row_count, 0)


def per_device(
    tokens,
    gain_attn,
    gain_ffn,
    w_query,
    w_key,
    w_value,
    w_out,
    w_in,
    w_down,
    segment_ids,
    cotangent,
):
    micro_count = tokens.shape[0]
    half_rows = tokens.shape[1]
    shard_list = (w_query, w_key, w_value, w_out, w_in, w_down)
    totals = tuple((jnp.zeros(shard.shape, jnp.float32) for shard in shard_list))
    gain_attn_total = jnp.zeros(gain_attn.shape, jnp.float32)
    gain_ffn_total = jnp.zeros(gain_ffn.shape, jnp.float32)
    outputs = []
    grad_rows = []
    for micro_idx in range(micro_count):
        weights = (
            lax.all_gather(w_query, "fsdp", axis=0, tiled=True),
            lax.all_gather(w_key, "fsdp", axis=0, tiled=True),
            lax.all_gather(w_value, "fsdp", axis=0, tiled=True),
            lax.all_gather(w_out, "fsdp", axis=1, tiled=True),
            lax.all_gather(w_in, "fsdp", axis=0, tiled=True),
            lax.all_gather(w_down, "fsdp", axis=1, tiled=True),
        )
        wq_all, wk_all, wv_all, wo_all, win_all, wdown_all = weights
        rows_in = tokens[micro_idx].astype(jnp.float32)
        cot_rows = cotangent[micro_idx]
        permitted_mask = block_mask(segment_ids[micro_idx])
        normed, norm_back = jax.vjp(layer_norm, rows_in, gain_attn)
        normed_own = normed.astype(jnp.bfloat16)
        normed_all = lax.all_gather(normed_own, "tp", axis=0, tiled=True)
        length = normed_all.shape[0]
        query_rows = product(normed_all, wq_all).astype(jnp.bfloat16)
        incoming_keys = product(normed_all, wk_all).astype(jnp.bfloat16)
        incoming_values = product(normed_all, wv_all).astype(jnp.bfloat16)

        def to_heads(values):
            return values.astype(jnp.float32).reshape(length, -1, HEAD_DIM).transpose(1, 0, 2)

        def joined(values):
            return values.transpose(1, 0, 2).reshape(length, -1)

        def attend(per_head_query, per_head_keys, per_head_values):
            return balanced_transport_kernel(
                per_head_query, per_head_keys, per_head_values, permitted_mask, quantized_result
            )

        mixture_h, attend_back = jax.vjp(
            attend, to_heads(query_rows), to_heads(incoming_keys), to_heads(incoming_values)
        )
        mixture_full = joined(mixture_h).astype(jnp.bfloat16)
        attended = lax.psum_scatter(
            product(
                row_slice(mixture_full, jnp.int32(0), half_rows * lax.axis_size("tp")), wo_all
            ).astype(jnp.bfloat16),
            "tp",
            scatter_dimension=0,
            tiled=True,
        ).astype(jnp.float32)
        middle = rows_in + attended
        normed_ffn, norm_ffn_back = jax.vjp(layer_norm, middle, gain_ffn)
        ffn_input, cot_all = (
            lax.all_gather(normed_ffn.astype(jnp.bfloat16), "tp", axis=0, tiled=True),
            lax.all_gather(cot_rows, "tp", axis=0, tiled=True),
        )
        hidden_pre = product(ffn_input, win_all)
        hidden_val, gelu_back = jax.vjp(partial(jax.nn.gelu, approximate=True), hidden_pre)
        hidden = hidden_val.astype(jnp.bfloat16)
        ffn_out = lax.psum_scatter(
            product(
                row_slice(hidden, jnp.int32(0), half_rows * lax.axis_size("tp")), wdown_all
            ).astype(jnp.bfloat16),
            "tp",
            scatter_dimension=0,
            tiled=True,
        ).astype(jnp.float32)
        outputs.append((middle + ffn_out).astype(jnp.bfloat16))
        grad_down = inner_rows(hidden, cot_all)
        grad_hidden = outer_cols(cot_all, wdown_all)
        grad_pre = gelu_back(grad_hidden)[0].astype(jnp.bfloat16)
        grad_in = inner_rows(ffn_input, grad_pre)
        grad_normed_ffn = lax.psum_scatter(
            outer_cols(
                row_slice(grad_pre, jnp.int32(0), half_rows * lax.axis_size("tp")), win_all
            ).astype(jnp.bfloat16),
            "tp",
            scatter_dimension=0,
            tiled=True,
        ).astype(jnp.float32)
        grad_mid_norm, grad_gain_ffn = norm_ffn_back(grad_normed_ffn)
        grad_middle = cot_rows.astype(jnp.float32) + grad_mid_norm
        grad_attended = lax.all_gather(grad_middle.astype(jnp.bfloat16), "tp", axis=0, tiled=True)
        grad_mixture = outer_cols(grad_attended, wo_all)
        grad_out = inner_rows(mixture_full, grad_attended)
        grad_query_h, grad_keys_h, grad_values_h = attend_back(to_heads(grad_mixture))
        grad_queries = joined(grad_query_h).astype(jnp.bfloat16)
        grad_keys = joined(grad_keys_h).astype(jnp.bfloat16)
        grad_values = joined(grad_values_h).astype(jnp.bfloat16)
        grad_wq = inner_rows(normed_all, grad_queries)
        grad_wk = inner_rows(normed_all, grad_keys)
        grad_wv = inner_rows(normed_all, grad_values)
        first_row = jnp.int32(0)
        total_term = outer_cols(
            row_slice(grad_queries, first_row, half_rows * lax.axis_size("tp")), wq_all
        )
        total_term = total_term + outer_cols(
            row_slice(grad_keys, first_row, half_rows * lax.axis_size("tp")), wk_all
        )
        grad_normed = lax.psum_scatter(
            (
                total_term
                + outer_cols(
                    row_slice(grad_values, first_row, half_rows * lax.axis_size("tp")), wv_all
                )
            ).astype(jnp.bfloat16),
            "tp",
            scatter_dimension=0,
            tiled=True,
        ).astype(jnp.float32)
        grad_rows_norm, grad_gain_attn = norm_back(grad_normed)
        grad_rows.append((grad_middle + grad_rows_norm).astype(jnp.bfloat16))
        gain_attn_total = gain_attn_total + grad_gain_attn
        gain_ffn_total = gain_ffn_total + grad_gain_ffn
        shares = (
            lax.psum_scatter(grad_wq, "fsdp", scatter_dimension=0, tiled=True),
            lax.psum_scatter(grad_wk, "fsdp", scatter_dimension=0, tiled=True),
            lax.psum_scatter(grad_wv, "fsdp", scatter_dimension=0, tiled=True),
            lax.psum_scatter(grad_out, "fsdp", scatter_dimension=1, tiled=True),
            lax.psum_scatter(grad_in, "fsdp", scatter_dimension=0, tiled=True),
            lax.psum_scatter(grad_down, "fsdp", scatter_dimension=1, tiled=True),
        )
        totals = tuple((a + b for a, b in zip(totals, shares)))
    gain_shares = (
        lax.psum_scatter(gain_attn_total, ("fsdp", "tp"), scatter_dimension=0, tiled=True),
        lax.psum_scatter(gain_ffn_total, ("fsdp", "tp"), scatter_dimension=0, tiled=True),
    )
    return (
        jnp.stack(outputs),
        jnp.stack(grad_rows),
        gain_shares[0],
        gain_shares[1],
        totals[0],
        totals[1],
        totals[2],
        totals[3],
        totals[4],
        totals[5],
    )


def solution(mesh):
    return jax.shard_map(
        per_device,
        mesh=mesh,
        in_specs=(
            P(None, ("fsdp", "tp"), None),
            P(),
            P(),
            P("fsdp", "tp"),
            P("fsdp", "tp"),
            P("fsdp", "tp"),
            P("tp", "fsdp"),
            P("fsdp", "tp"),
            P("tp", "fsdp"),
            P(None, "fsdp"),
            P(None, ("fsdp", "tp"), None),
        ),
        out_specs=(
            P(None, ("fsdp", "tp"), None),
            P(None, ("fsdp", "tp"), None),
            P(("fsdp", "tp")),
            P(("fsdp", "tp")),
            P("fsdp", "tp"),
            P("fsdp", "tp"),
            P("fsdp", "tp"),
            P("tp", "fsdp"),
            P("fsdp", "tp"),
            P("tp", "fsdp"),
        ),
        check_vma=False,
    )
```

profile of v0, /device:TPU:0, one launch (start us, length us, event | category | flops | bytes accessed | tf_op | source)
XLA Modules:
  0.0 1168.4 jit_solution(16473712469427519521)
XLA Ops:
  13.1 43.8 %all_gather.50 = bf16[512,256]{1,0:T(8,128)(2,1)S(1)} all-gather(bf16[32,256]{1,0:T(8,128)(2,1)S(1)} %copy-done.293), channel_id=1, replica_groups=mesh['fsdp'=16,'tp'=2] {'fsdp'}, dimensions={0}, use_global_device_ids=true | all-gather | bytes 278528 | tf_op jit(solution)/shard_map/all_gather | solution.py:120
  56.9 36.8 %all_gather.49 = bf16[512,256]{1,0:T(8,128)(2,1)S(1)} all-gather(bf16[32,256]{1,0:T(8,128)(2,1)S(1)} %copy-done.294), channel_id=1, replica_groups=mesh['fsdp'=16,'tp'=2] {'fsdp'}, dimensions={0}, use_global_device_ids=true | all-gather | bytes 278528 | tf_op jit(solution)/shard_map/all_gather | solution.py:119
  93.7 41.2 %all_gather.51 = bf16[512,256]{1,0:T(8,128)(2,1)} all-gather(bf16[32,256]{1,0:T(8,128)(2,1)S(1)} %copy-done.295), channel_id=1, replica_groups=mesh['fsdp'=16,'tp'=2] {'fsdp'}, dimensions={0}, use_global_device_ids=true | all-gather | bytes 278528 | tf_op jit(solution)/shard_map/all_gather | solution.py:121
  135.0 39.3 %all_gather.52 = bf16[256,512]{0,1:T(8,128)(2,1)} all-gather(bf16[256,32]{0,1:T(8,128)(2,1)S(1)} %copy-done.296), channel_id=1, replica_groups=mesh['fsdp'=16,'tp'=2] {'fsdp'}, dimensions={1}, use_global_device_ids=true | all-gather | bytes 278528 | tf_op jit(solution)/shard_map/all_gather | solution.py:122
  200.2 3.0 fusion.349
  209.8 3.5 add_convert_fusion.5
  215.3 6.2 reduce-scatter.15.cloned.1.call-done
  225.2 9.8 all-gather.21.cloned.1.call-done
  235.0 2.6 convolution_convert_fusion.7
  268.9 3.2 fusion.354
  278.2 4.6 add_convert_fusion.4
  284.4 2.6 convolution_convert_fusion.3
  287.8 9.2 reduce-scatter.19.cloned.1.call-done
  306.0 40.9 %all-gather.17.cloned.1.call-done = bf16[512,1024]{1,0:T(8,128)(2,1)} async-done(((bf16[32,1024]{1,0:T(8,128)(2,1)}), bf16[512,1024]{1,0:T(8,128)(2,1)}) %all-gather.17.cloned.1.call-update) | async-done | bytes 1048592 | tf_op jit(solution)/shard_map/all_gather | solution.py:123
  346.9 9.2 all-gather.23.cloned.1.call-done
  356.1 4.7 fusion.359
  360.8 6.8 all-gather.31.cloned.1.call-done
  367.6 59.4 %all-gather.19.cloned.1.call-done = bf16[1024,512]{0,1:T(8,128)(2,1)} async-done(((bf16[1024,32]{0,1:T(8,128)(2,1)}), bf16[1024,512]{0,1:T(8,128)(2,1)}) %all-gather.19.cloned.1.call-update) | async-done | bytes 1048592 | tf_op jit(solution)/shard_map/all_gather | solution.py:124
  427.0 6.2 fusion.13
  437.0 4.8 fusion.358
  441.8 6.5 all-gather.29.cloned.1.call-done
  448.2 6.2 fusion.6
  458.2 5.1 convolution_convert_fusion.4
  463.3 5.3 convolution_convert_fusion.2
  468.8 3.0 fusion.160
  474.1 5.8 reduce-scatter.17.cloned.1.call-done
  480.0 12.1 %reduce-scatter.21.cloned.1.call-done = bf16[512,512]{1,0:T(8,128)(2,1)} async-done(((bf16[1024,512]{1,0:T(8,128)(2,1)}), bf16[512,512]{1,0:T(8,128)(2,1)}) %reduce-scatter.21.cloned.1.call-update) | async-done | bytes 524304 | tf_op jit(solution)/shard_map/reduce_scatter | solution.py:170
  492.1 3.3 fusion.332
  498.7 8.6 all-gather.27.cloned.1.call-done
  507.2 2.7 fusion.364
  511.8 5.9 fusion.24
  517.7 3.2 fusion.132
  521.0 4.4 fusion.44
  525.4 3.3 fusion.365
  528.7 5.9 fusion.56
  534.6 2.7 fusion.360
  537.4 3.1 copy.141
  540.5 6.7 fusion.32
  547.2 4.5 fusion.63
  553.7 4.4 fusion.52
  558.1 2.6 fusion.126
  567.4 4.4 fusion.40
  571.8 2.6 fusion.357
  581.3 4.4 fusion.48
  586.1 2.6 fusion.356
  597.6 5.1 fusion.59
  602.8 5.6 fusion.18
  610.8 8.5 fusion.21
  619.4 3.8 fusion.20
  646.7 4.1 add_convert_fusion.1
  657.2 5.6 fusion.23
  668.7 5.1 fusion.66
  682.7 3.0 fusion.372
  685.7 2.6 convolution_add_fusion.1
  690.5 2.9 convolution_add_fusion.2
  702.4 4.4 fusion.166
  706.9 3.2 convolution_add_fusion
  716.9 42.0 %all-reduce.6 = (f32[512]{0:T(512)S(1)}, f32[512]{0:T(512)S(1)}) all-reduce(f32[512]{0:T(512)S(1)} %add.514, f32[512]{0:T(512)S(1)} %add.515), channel_id=18, replica_groups=mesh['fsdp'=16,'tp'=2] {'fsdp','tp'}, use_global_device_ids=true, to_apply=%region_134.135.clone | all-reduce | flops 1024 | bytes 8192
  763.6 12.9 %reduce-scatter.39.cloned.1.call-done = f32[32,1024]{1,0:T(8,128)} async-done(((f32[512,1024]{1,0:T(8,128)}), f32[32,1024]{1,0:T(8,128)}) %reduce-scatter.39.cloned.1.call-update) | async-done | bytes 131088 | tf_op jit(solution)/shard_map/reduce_scatter | solution.py:230
  776.5 76.9 %reduce-scatter.37.cloned.1.call-done = f32[256,32]{0,1:T(8,128)} async-done(((f32[256,512]{0,1:T(8,128)}), f32[256,32]{0,1:T(8,128)}) %reduce-scatter.37.cloned.1.call-update) | async-done | bytes 32784 | tf_op jit(solution)/shard_map/reduce_scatter | solution.py:229
  853.4 75.7 %reduce-scatter.35.cloned.1.call-done = f32[32,256]{1,0:T(8,128)} async-done(((f32[512,256]{1,0:T(8,128)}), f32[32,256]{1,0:T(8,128)}) %reduce-scatter.35.cloned.1.call-update) | async-done | bytes 32784 | tf_op jit(solution)/shard_map/reduce_scatter | solution.py:228
  929.0 75.8 %reduce-scatter.33.cloned.1.call-done = f32[32,256]{1,0:T(8,128)} async-done(((f32[512,256]{1,0:T(8,128)}), f32[32,256]{1,0:T(8,128)}) %reduce-scatter.33.cloned.1.call-update) | async-done | bytes 32784 | tf_op jit(solution)/shard_map/reduce_scatter | solution.py:227
  1004.8 75.8 %reduce-scatter.31.cloned.1.call-done = f32[32,256]{1,0:T(8,128)} async-done(((f32[512,256]{1,0:T(8,128)}), f32[32,256]{1,0:T(8,128)}) %reduce-scatter.31.cloned.1.call-update) | async-done | bytes 32784 | tf_op jit(solution)/shard_map/reduce_scatter | solution.py:226
  1080.6 79.7 %reduce-scatter.41.cloned.1.call-done = f32[1024,32]{0,1:T(8,128)} async-done(((f32[1024,512]{0,1:T(8,128)}), f32[1024,32]{0,1:T(8,128)}) %reduce-scatter.41.cloned.1.call-update) | async-done | bytes 131088 | tf_op jit(solution)/shard_map/reduce_scatter | solution.py:231
  (1001 shorter events, 196.6 us)
Async XLA Ops:
  8.0 48.9 %copy-start.294 = (bf16[32,256]{1,0:T(8,128)(2,1)S(1)}, bf16[32,256]{1,0:T(8,128)(2,1)}, u32[]{:S(2)}) copy-start(bf16[32,256]{1,0:T(8,128)(2,1)} %param.14) | copy-start | bytes 49156
  8.0 85.7 %copy-start.295 = (bf16[32,256]{1,0:T(8,128)(2,1)S(1)}, bf16[32,256]{1,0:T(8,128)(2,1)}, u32[]{:S(2)}) copy-start(bf16[32,256]{1,0:T(8,128)(2,1)} %param.16) | copy-start | bytes 49156
  8.0 126.9 %copy-start.296 = (bf16[256,32]{0,1:T(8,128)(2,1)S(1)}, bf16[256,32]{0,1:T(8,128)(2,1)}, u32[]{:S(2)}) copy-start(bf16[256,32]{0,1:T(8,128)(2,1)} %param.17) | copy-start | bytes 49156
  8.1 168.0 %all-gather.13.cloned.1.call-start = ((), (), s32[]{:S(2)}) async-start(), calls=%async_computation.14 | async-start | bytes 1572864 | tf_op jit(solution)/shard_map/all_gather | solution.py:132
  8.1 166.2 %copy-start.300 = (s32[2,32]{1,0:T(2,128)S(1)}, s32[2,32]{1,0:T(2,128)}, u32[]{:S(2)}) copy-start(s32[2,32]{1,0:T(2,128)} %param.20) | copy-start | bytes 772
  9.5 166.4 %copy-start.163 = (f32[512]{0:T(512)}, f32[512]{0:T(512)S(1)}, u32[]{:S(2)}) copy-start(f32[512]{0:T(512)S(1)} %broadcast_multiply_fusion.3) | copy-start | bytes 6148
  10.9 165.1 %copy-start.229 = (f32[512]{0:T(512)}, f32[512]{0:T(512)S(1)}, u32[]{:S(2)}) copy-start(f32[512]{0:T(512)S(1)} %fusion.156) | copy-start | bytes 6148
  10.9 165.1 %copy-start.204 = (f32[512]{0:T(512)}, f32[512]{0:T(512)S(1)}, u32[]{:S(2)}) copy-start(f32[512]{0:T(512)S(1)} %fusion.287) | copy-start | bytes 6148
  13.0 208.5 %reduce-scatter.15.cloned.1.call-start = ((), (), s32[]{:S(2)}) async-start(), calls=%async_computation.15 | async-start | bytes 1572864 | tf_op jit(solution)/shard_map/reduce_scatter | solution.py:153
  56.9 120.9 %copy-start.59 = (bf16[512,256]{1,0:T(8,128)(2,1)}, bf16[512,256]{1,0:T(8,128)(2,1)S(1)}, u32[]{:S(2)}) copy-start(bf16[512,256]{1,0:T(8,128)(2,1)S(1)} %all_gather.50) | copy-start | bytes 786436
  93.7 85.0 %copy-start.56 = (bf16[512,256]{1,0:T(8,128)(2,1)}, bf16[512,256]{1,0:T(8,128)(2,1)S(1)}, u32[]{:S(2)}) copy-start(bf16[512,256]{1,0:T(8,128)(2,1)S(1)} %all_gather.49) | copy-start | bytes 786436
  135.0 68.2 %copy-start.144 = (pred[32,32]{1,0:T(8,128)(4,1)}, pred[32,32]{1,0:T(8,128)(4,1)S(1)}, u32[]{:S(2)}) copy-start(pred[32,32]{1,0:T(8,128)(4,1)S(1)} %iota_compare_fusion.1) | copy-start | bytes 3076
  178.3 24.9 %copy-start.17 = (bf16[1024,4,64]{2,0,1:T(8,128)(2,1)}, bf16[1024,4,64]{2,0,1:T(8,128)(2,1)S(1)}, u32[]{:S(2)}) copy-start(bf16[1024,4,64]{2,0,1:T(8,128)(2,1)S(1)} %copy.126) | copy-start | bytes 1572868
  181.6 21.6 %copy-start.20 = (bf16[4,1024,64]{2,1,0:T(8,128)(2,1)}, bf16[4,1024,64]{2,1,0:T(8,128)(2,1)S(1)}, u32[]{:S(2)}) copy-start(bf16[4,1024,64]{2,1,0:T(8,128)(2,1)S(1)} %copy.125) | copy-start | bytes 1572868
  181.6 13.0 %copy-start.51 = (bf16[512,256]{1,0:T(8,128)(2,1)S(1)}, bf16[512,256]{1,0:T(8,128)(2,1)}, u32[]{:S(2)}) copy-start(bf16[512,256]{1,0:T(8,128)(2,1)} %all_gather.51) | copy-start | bytes 786436
  182.0 13.8 %copy-start.130 = (f32[4,32,64]{2,1,0:T(8,128)}, f32[4,32,64]{2,1,0:T(8,128)S(1)}, u32[]{:S(2)}) copy-start(f32[4,32,64]{2,1,0:T(8,128)S(1)} %convert_reduce_fusion.3) | copy-start | bytes 98308
  184.7 12.7 %copy-start.90 = (f32[4,32]{1,0:T(4,128)}, f32[4,32]{1,0:T(4,128)S(1)}, u32[]{:S(2)}) copy-start(f32[4,32]{1,0:T(4,128)S(1)} %log_add_fusion.29) | copy-start | bytes 1540
  185.6 11.8 %copy-start.108 = (f32[4,32]{1,0:T(4,128)}, f32[4,32]{1,0:T(4,128)S(1)}, u32[]{:S(2)}) copy-start(f32[4,32]{1,0:T(4,128)S(1)} %log_add_fusion.28) | copy-start | bytes 1540
  215.2 19.8 %copy-start.60 = (bf16[512,256]{1,0:T(8,128)(2,1)S(1)}, bf16[512,256]{1,0:T(8,128)(2,1)}, u32[]{:S(2)}) copy-start(bf16[512,256]{1,0:T(8,128)(2,1)} %copy-done.59) | copy-start | bytes 786436
  215.2 19.8 %all-gather.21.cloned.1.call-start = ((), (), s32[]{:S(2)}) async-start(), calls=%async_computation.20 | async-start | bytes 1572864 | tf_op jit(solution)/shard_map/all_gather | solution.py:132
  215.3 22.3 %copy-start.165 = (f32[512]{0:T(512)}, f32[512]{0:T(512)S(1)}, u32[]{:S(2)}) copy-start(f32[512]{0:T(512)S(1)} %broadcast_multiply_fusion.1) | copy-start | bytes 6148
  223.6 14.0 %copy-start.231 = (f32[512]{0:T(512)}, f32[512]{0:T(512)S(1)}, u32[]{:S(2)}) copy-start(f32[512]{0:T(512)S(1)} %get-tuple-element.27) | copy-start | bytes 6148
  223.6 14.0 %copy-start.206 = (f32[512]{0:T(512)}, f32[512]{0:T(512)S(1)}, u32[]{:S(2)}) copy-start(f32[512]{0:T(512)S(1)} %fusion.289) | copy-start | bytes 6148
  224.6 72.3 %reduce-scatter.19.cloned.1.call-start = ((), (), s32[]{:S(2)}) async-start(), calls=%async_computation.21 | async-start | bytes 1572864 | tf_op jit(solution)/shard_map/reduce_scatter | solution.py:153
  225.2 20.7 %copy-start.298 = (pred[32,32]{1,0:T(8,128)(4,1)}, pred[32,32]{1,0:T(8,128)(4,1)S(1)}, u32[]{:S(2)}) copy-start(pred[32,32]{1,0:T(8,128)(4,1)S(1)} %fusion.280) | copy-start | bytes 3076
  239.1 28.5 %copy-start.22 = (bf16[1024,4,64]{2,0,1:T(8,128)(2,1)}, bf16[1024,4,64]{2,0,1:T(8,128)(2,1)S(1)}, u32[]{:S(2)}) copy-start(bf16[1024,4,64]{2,0,1:T(8,128)(2,1)S(1)} %copy.134) | copy-start | bytes 1572868
  244.2 17.4 %copy-start.52 = (bf16[512,256]{1,0:T(8,128)(2,1)S(1)}, bf16[512,256]{1,0:T(8,128)(2,1)}, u32[]{:S(2)}) copy-start(bf16[512,256]{1,0:T(8,128)(2,1)} %all_gather.51) | copy-start | bytes 786436
  282.8 14.1 %copy-start.42 = (bf16[512,512]{1,0:T(8,128)(2,1)S(1)}, bf16[512,512]{1,0:T(8,128)(2,1)}, u32[]{:S(2)}) copy-start(bf16[512,512]{1,0:T(8,128)(2,1)} %reduce-scatter.15.cloned.1.call-done) | copy-start | bytes 1572868
  287.1 59.8 %all-gather.17.cloned.1.call-start = ((), (), s32[]{:S(2)}) async-start(), calls=%async_computation.17 | async-start | bytes 1114112 | tf_op jit(solution)/shard_map/all_gather | solution.py:123
  287.7 68.4 %all-gather.23.cloned.1.call-start = ((), (), s32[]{:S(2)}) async-start(), calls=%async_computation.22 | async-start | bytes 1572864 | tf_op jit(solution)/shard_map/all_gather | solution.py:164
  302.2 65.5 %all-gather.31.cloned.1.call-start = ((), (), s32[]{:S(2)}) async-start(), calls=%async_computation.31 | async-start | bytes 1572864 | tf_op jit(solution)/shard_map/all_gather | solution.py:165
  303.3 123.7 %all-gather.19.cloned.1.call-start = ((), (), s32[]{:S(2)}) async-start(), calls=%async_computation.18 | async-start | bytes 1114112 | tf_op jit(solution)/shard_map/all_gather | solution.py:124
  304.0 133.0 %all-gather.15.cloned.1.call-start = ((), (), s32[]{:S(2)}) async-start(), calls=%async_computation.16 | async-start | bytes 1572864 | tf_op jit(solution)/shard_map/all_gather | solution.py:164
  304.8 143.5 %all-gather.29.cloned.1.call-start = ((), (), s32[]{:S(2)}) async-start(), calls=%async_computation.30 | async-start | bytes 1572864 | tf_op jit(solution)/shard_map/all_gather | solution.py:165
  305.5 163.2 %reduce-scatter.27.cloned.1.call-start = ((), (), s32[]{:S(2)}) async-start(), calls=%async_computation.27 | async-start | bytes 1572864 | tf_op jit(solution)/shard_map/reduce_scatter | solution.py:183
  436.9 31.8 %reduce-scatter.23.cloned.1.call-start = ((), (), s32[]{:S(2)}) async-start(), calls=%async_computation.24 | async-start | bytes 1572864 | tf_op jit(solution)/shard_map/reduce_scatter | solution.py:183
  458.1 21.9 %reduce-scatter.17.cloned.1.call-start = ((), (), s32[]{:S(2)}) async-start(), calls=%async_computation.19 | async-start | bytes 1572864 | tf_op jit(solution)/shard_map/reduce_scatter | solution.py:170
  463.3 28.8 %reduce-scatter.21.cloned.1.call-start = ((), (), s32[]{:S(2)}) async-start(), calls=%async_computation.23 | async-start | bytes 1572864 | tf_op jit(solution)/shard_map/reduce_scatter | solution.py:170
  468.7 38.6 %all-gather.27.cloned.1.call-start = ((), (), s32[]{:S(2)}) async-start(), calls=%async_computation.28 | async-start | bytes 1572864 | tf_op jit(solution)/shard_map/all_gather | solution.py:193
  495.4 11.8 %copy-start.55 = (bf16[256,512]{0,1:T(8,128)(2,1)S(1)}, bf16[256,512]{0,1:T(8,128)(2,1)}, u32[]{:S(2)}) copy-start(bf16[256,512]{0,1:T(8,128)(2,1)} %all_gather.52) | copy-start | bytes 786436
  497.1 37.6 %all-gather.25.cloned.1.call-start = ((), (), s32[]{:S(2)}) async-start(), calls=%async_computation.25 | async-start | bytes 1572864 | tf_op jit(solution)/shard_map/all_gather | solution.py:193
  498.4 214.0 %reduce-scatter.29.cloned.1.call-start = ((), (), s32[]{:S(2)}) async-start(), calls=%async_computation.29 | async-start | bytes 1572864 | tf_op jit(solution)/shard_map/reduce_scatter | solution.py:210
  564.8 32.9 %copy-start.11 = (f32[4,32,32,64]{3,2,1,0:T(8,128)}, f32[4,32,32,64]{3,2,1,0:T(8,128)S(1)}, u32[]{:S(2)}) copy-start(f32[4,32,32,64]{3,2,1,0:T(8,128)S(1)} %add_multiply_fusion) | copy-start | bytes 3145732
  623.2 11.3 copy-start.91
  623.2 11.3 copy-start.109
  623.2 11.3 copy-start.124
  623.2 11.4 copy-start.141
  623.3 11.4 copy-start.154
  623.3 11.4 copy-start.177
  623.3 12.2 %copy-start.188 = (f32[4,32]{1,0:T(4,128)S(1)}, f32[4,32]{1,0:T(4,128)}, u32[]{:S(2)}) copy-start(f32[4,32]{1,0:T(4,128)} %copy-done.187) | copy-start | bytes 1540
  625.7 21.0 %copy-start.24 = (bf16[1024,4,64]{2,0,1:T(8,128)(2,1)S(1)}, bf16[1024,4,64]{2,0,1:T(8,128)(2,1)}, u32[]{:S(2)}) copy-start(bf16[1024,4,64]{2,0,1:T(8,128)(2,1)} %copy-done.22) | copy-start | bytes 1572868
  625.7 21.0 %copy-start.147 = (pred[32,32]{1,0:T(8,128)(4,1)S(1)}, pred[32,32]{1,0:T(8,128)(4,1)}, u32[]{:S(2)}) copy-start(pred[32,32]{1,0:T(8,128)(4,1)} %copy-done.144) | copy-start | bytes 3076
  625.7 21.0 %copy-start.180 = (f32[4,32,64]{2,1,0:T(8,128)S(1)}, f32[4,32,64]{2,1,0:T(8,128)}, u32[]{:S(2)}) copy-start(f32[4,32,64]{2,1,0:T(8,128)} %convolution_multiply_fusion.1) | copy-start | bytes 98308
  656.8 55.7 %reduce-scatter.25.cloned.1.call-start = ((), (), s32[]{:S(2)}) async-start(), calls=%async_computation.26 | async-start | bytes 1572864 | tf_op jit(solution)/shard_map/reduce_scatter | solution.py:210
  682.3 94.2 %reduce-scatter.39.cloned.1.call-start = ((), (), s32[]{:S(2)}) async-start(), calls=%async_computation.36 | async-start | bytes 2228224 | tf_op jit(solution)/shard_map/reduce_scatter | solution.py:230
  688.4 165.0 %reduce-scatter.37.cloned.1.call-start = ((), (), s32[]{:S(2)}) async-start(), calls=%async_computation.35 | async-start | bytes 557056 | tf_op jit(solution)/shard_map/reduce_scatter | solution.py:229
  693.4 235.6 %reduce-scatter.35.cloned.1.call-start = ((), (), s32[]{:S(2)}) async-start(), calls=%async_computation.34 | async-start | bytes 557056 | tf_op jit(solution)/shard_map/reduce_scatter | solution.py:228
  696.4 308.4 %reduce-scatter.33.cloned.1.call-start = ((), (), s32[]{:S(2)}) async-start(), calls=%async_computation.33 | async-start | bytes 557056 | tf_op jit(solution)/shard_map/reduce_scatter | solution.py:227
  699.4 381.2 %reduce-scatter.31.cloned.1.call-start = ((), (), s32[]{:S(2)}) async-start(), calls=%async_computation.32 | async-start | bytes 557056 | tf_op jit(solution)/shard_map/reduce_scatter | solution.py:226
  702.4 457.9 %reduce-scatter.41.cloned.1.call-start = ((), (), s32[]{:S(2)}) async-start(), calls=%async_computation.37 | async-start | bytes 2228224 | tf_op jit(solution)/shard_map/reduce_scatter | solution.py:231
  712.4 47.7 %copy-start.45 = (bf16[2,512,512]{2,1,0:T(8,128)(2,1)S(1)}, bf16[2,512,512]{2,1,0:T(8,128)(2,1)}, u32[]{:S(2)}) copy-start(bf16[2,512,512]{2,1,0:T(8,128)(2,1)} %param.21) | copy-start | bytes 3145732
  712.4 47.7 %copy-start.47 = (f32[512,512]{1,0:T(8,128)S(1)}, f32[512,512]{1,0:T(8,128)}, u32[]{:S(2)}) copy-start(f32[512,512]{1,0:T(8,128)} %copy-done.46) | copy-start | bytes 3145732
  712.4 47.7 %copy-start.225 = (f32[512]{0:T(512)S(1)}, f32[512]{0:T(512)}, u32[]{:S(2)}) copy-start(f32[512]{0:T(512)} %copy-done.224) | copy-start | bytes 6148
  712.4 47.7 %copy-start.227 = (f32[512]{0:T(512)S(1)}, f32[512]{0:T(512)}, u32[]{:S(2)}) copy-start(f32[512]{0:T(512)} %copy-done.226) | copy-start | bytes 6148
  (279 other events, 1088.3 us)
Sparse Core Ops, SparseCore 0:
  13.1 11.7 all-gather.12
  215.4 6.1 reduce-scatter.14
  224.8 10.1 all-gather.20
  287.2 9.6 reduce-scatter.18
  437.0 7.3 reduce-scatter.26
  458.2 9.7 reduce-scatter.22
  470.2 9.6 reduce-scatter.16
  482.3 9.6 reduce-scatter.20
Sparse Core Ops, SparseCore 1:
  290.3 56.5 all-gather.16
  348.3 7.7 all-gather.22
  357.5 10.1 all-gather.30
  370.4 56.5 all-gather.18
  428.7 7.7 all-gather.14
  438.1 10.1 all-gather.28
  497.1 10.0 all-gather.26
  508.6 10.1 all-gather.24
  656.9 9.7 reduce-scatter.28
  682.4 9.7 reduce-scatter.24
  694.9 81.6 reduce-scatter.38
  779.3 74.0 reduce-scatter.36
  856.2 72.8 reduce-scatter.34
  931.9 72.9 reduce-scatter.32
  1007.8 72.8 reduce-scatter.30
  1083.5 76.8 reduce-scatter.40
where the time goes:
time: 1180 us; the launch traced here: 1170 us
  waiting for transfers between devices  574 us (49%)
  matrix products  222 us (19%)
  blocking collectives  203 us (17%)
  other arithmetic  87.4 us (7%)
  local copies, waits for them, and re-layouts  57.9 us (5%)
  between operations  21.4 us (2%)
    reduce_scatter x1, waiting for transfers between devices, per_device(): lax.psum_scatter(grad_down, 'fsdp', scatter_dimension=1, tiled=True)  79.7 us
    reduce_scatter x1, waiting for transfers between devices, per_device(): lax.psum_scatter(grad_out, 'fsdp', scatter_dimension=1, tiled=True)  76.9 us
    reduce_scatter x1, waiting for transfers between devices, per_device(): lax.psum_scatter(grad_wq, 'fsdp', scatter_dimension=0, tiled=True)  75.8 us
    reduce_scatter x1, waiting for transfers between devices, per_device(): lax.psum_scatter(grad_wk, 'fsdp', scatter_dimension=0, tiled=True)  75.8 us
    reduce_scatter x1, waiting for transfers between devices, per_device(): lax.psum_scatter(grad_wv, 'fsdp', scatter_dimension=0, tiled=True)  75.7 us
    all_gather x1, waiting for transfers between devices, per_device(): lax.all_gather(w_down, 'fsdp', axis=1, tiled=True)  59.4 us
    all_gather x1, blocking collectives, per_device(): lax.all_gather(w_key, 'fsdp', axis=0, tiled=True)  43.8 us
    unnamed x1, blocking collectives  42 us
  transfers between devices with their start and end apart: 24, of which 17 were waited for; matrix products, arithmetic and copies ran while one was open for 12% of the time, Pallas kernels for 0%

commit v1 on v0

v1 whole, which is shorter than its diff:
```python
import functools, math
import jax, jax.numpy as jnp
from jax import lax
from jax.experimental import pallas as pl
from jax.experimental.pallas import tpu as pltpu
from jax.sharding import PartitionSpec as P

F32, BF = jnp.float32, jnp.bfloat16
HI = lax.Precision.HIGHEST
HD, BLK, ITERS, NB, D, FF, T = 64, 32, 8, 32, 512, 2048, 1024
HALF = D // 2
COLS = 3 * HALF + HALF + FF
QO, KO, VO, OO, IO, DO = 0, 256, 512, 768, 1024, 2048


def nn(a, b, precision=None):
    return lax.dot_general(a, b, (((1,), (0,)), ((), ())), precision=precision, preferred_element_type=F32)


def nt(a, b, precision=None):
    return lax.dot_general(a, b, (((1,), (1,)), ((), ())), precision=precision, preferred_element_type=F32)


def tn(a, b, precision=None):
    return lax.dot_general(a, b, (((0,), (0,)), ((), ())), precision=precision, preferred_element_type=F32)


def iota(shape, dim):
    return lax.broadcasted_iota(jnp.int32, shape, dim)


def order_matrix(inverse):
    n, m = iota((128, 128), 0), iota((128, 128), 1)
    if inverse:
        n, m = m, n
    return (m == (n & 3) * 32 + (n >> 2)).astype(BF)


def norm_rows(x, gain):
    center = x - jnp.mean(x, axis=1, keepdims=True)
    inv = lax.rsqrt(jnp.mean(center * center, axis=1, keepdims=True) + 1e-05)
    xhat = center * inv
    return xhat, inv


def norm_back(xhat, inv, gain, grad):
    gx = grad * gain
    m1 = jnp.mean(gx, axis=1, keepdims=True)
    m2 = jnp.mean(gx * xhat, axis=1, keepdims=True)
    return inv * (gx - m1 - xhat * m2)


def even_lanes(shape):
    return (iota(shape, len(shape) - 1) & 127) < 64


def stack_heads(x):
    ev = even_lanes(x.shape)
    z = jnp.zeros_like(x)
    return jnp.concatenate([jnp.where(ev, x, z), jnp.where(ev, z, x)], axis=0)


def pick_heads(r):
    n = r.shape[0] // 2
    ev = even_lanes((n, r.shape[1]))
    return jnp.where(ev, r[:n], r[n:])


SCRATCH = dict(
    tokp=((T, D), BF), cotp=((T, D), BF), cott=((D, T), BF), nm=((T, D), BF), nmt=((D, T), BF),
    q=((T, D), BF), k=((T, D), BF), v=((T, D), BF), ks=((T, D), BF), vs=((T, D), BF),
    qm=((NB, D), F32), km=((NB, D), F32), sk=((2 * ITERS, 8 * NB, NB), F32), allow=((NB, NB), F32),
    kr=((8, 128, 128), BF), krt=((8, 128, 128), BF), bias=((128, 256), F32),
    pr=((4, 8, 256, 256), BF), mix=((T, D), BF), mid=((T, D), F32), nf=((T, D), BF), nft=((D, T), BF),
    hid=((T, 512), BF), gp=((T, 512), BF), res=((T, D), F32), gnf=((T, D), F32),
    ga=((T, D), BF), gat=((D, T), BF), gmix=((T, D), BF),
    dq=((T, D), F32), dk=((T, D), F32), dv=((T, D), F32), dks=((T, D), BF), dvs=((T, D), BF),
    dqb=((T, D), BF), dkb=((T, D), BF), dvb=((T, D), BF), ds=((8 * NB, NB), F32),
    gg=((8, D), F32),
)


def loop(n, body, unroll=1):
    lax.fori_loop(0, n, lambda i, c: (body(i), c)[1], 0, unroll=unroll)


def rows(i, n):
    return pl.ds(pl.multiple_of(i * n, n), n)


def st_tokens(s, tok, gain_attn):
    pm = order_matrix(False)

    def body(c):
        x = nn(pm, tok[rows(c, 128), :])
        s.tokp[rows(c, 128), :] = x.astype(BF)
        xhat, _ = norm_rows(x, None)
        s.nm[rows(c, 128), :] = (xhat * gain_attn[...]).astype(BF)
    loop(8, body)


def st_cot(s, cot):
    pm = order_matrix(False)

    def body(c):
        s.cotp[rows(c, 128), :] = nn(pm, cot[rows(c, 128), :]).astype(BF)
    loop(8, body)


def transpose_into(dst, src):
    for c in range(4):
        dst[:, c * 256:(c + 1) * 256] = jnp.transpose(src[c * 256:(c + 1) * 256, :], (1, 0))


def block_sums(x):
    y = jnp.sum(x.reshape(16, 8, x.shape[1]), axis=0)
    return y[0:4] + y[4:8]


def st_qkv(s, w):
    def body(m):
        x = s.nm[rows(m, 256), :]
        for t in range(2):
            out = nn(x, w[t, :, 0:768]).astype(BF)
            cs = slice(t * 256, (t + 1) * 256)
            qv, kv = out[:, 0:256], out[:, 256:512]
            s.q[rows(m, 256), cs] = qv
            s.k[rows(m, 256), cs] = kv
            s.v[rows(m, 256), cs] = out[:, 512:768]
            for ref, val in ((s.qm, qv), (s.km, kv)):
                val = val.astype(F32)
                sums = jnp.concatenate([block_sums(val[:128]), block_sums(val[128:])], axis=0)
                ref[rows(m, 8), cs] = sums * (1.0 / BLK)
    loop(4, body)


def st_sinkhorn(s, seg):
    row = jnp.broadcast_to(seg[...], (NB, NB))
    ri, ci = iota((NB, NB), 0), iota((NB, NB), 1)
    col = jnp.sum(jnp.where(ri == ci, row, 0), axis=1, keepdims=True)
    allow = ((row == col) & (ci <= ri)) | ((row == 0) & (col > 0))
    s.allow[...] = allow.astype(F32)
    parts = []
    for p in range(4):
        cs = slice(p * 128, (p + 1) * 128)
        parts.append(nt(stack_heads(s.qm[:, cs]), s.km[:, cs], precision=HI))
    x = jnp.concatenate(parts, axis=0) * (BLK / math.sqrt(HD))
    mask = jnp.concatenate([allow.astype(F32)] * 8, axis=0) > 0
    x = jnp.where(mask, x, -1000000000.0)
    for it in range(ITERS):
        m = jnp.max(x, axis=1, keepdims=True)
        e = jnp.exp(x - m)
        z = jnp.sum(e, axis=1, keepdims=True)
        s.sk[2 * it] = e * (1.0 / z)
        x = x - (m + jnp.log(z))
        y = x.reshape(8, NB, NB)
        m = jnp.max(y, axis=1, keepdims=True)
        e = jnp.exp(y - m)
        z = jnp.sum(e, axis=1, keepdims=True)
        s.sk[2 * it + 1] = (e * (1.0 / z)).reshape(8 * NB, NB)
        x = (y - (m + jnp.log(z))).reshape(8 * NB, NB)
    sorter = s.sk[2 * ITERS - 1].astype(BF)
    n = iota((128, NB), 0)
    e_mat = (((n >> 4) * 4 + (n & 3)) == iota((128, NB), 1)).astype(BF)
    wide = nt(sorter, e_mat).astype(BF)
    a, b = iota((128, 128), 0), iota((128, 128), 1)
    same = ((a >> 2) & 3) == ((b >> 2) & 3)
    for h in range(8):
        kr = jnp.where(same, nn(e_mat, wide[h * NB:(h + 1) * NB]), 0.0)
        s.kr[h] = kr.astype(BF)
        s.krt[h] = jnp.transpose(kr, (1, 0)).astype(BF)


def gather_chunk(ref, rq, cs):
    return jnp.concatenate([ref[pl.ds(pl.multiple_of(i * 128 + rq * 16, 16), 16), cs] for i in range(8)], axis=0)


def split_pair(x):
    return stack_heads(x)


def st_sort(s):
    def body(rq):
        for p in range(4):
            cs = slice(p * 128, (p + 1) * 128)
            kv = jnp.concatenate([gather_chunk(s.k, rq, cs), gather_chunk(s.v, rq, cs)], axis=1)
            lhs = jnp.concatenate([s.kr[2 * p], s.kr[2 * p + 1]], axis=1)
            out = nn(lhs, split_pair(kv)).astype(BF)
            for i in range(8):
                at = pl.ds(pl.multiple_of(i * 128 + rq * 16, 16), 16)
                s.ks[at, cs] = out[i * 16:(i + 1) * 16, 0:128]
                s.vs[at, cs] = out[i * 16:(i + 1) * 16, 128:256]
    loop(8, body)


def st_bias(s):
    n, m = iota((128, 256), 0), iota((128, 256), 1)
    ok = ((n & 3) == (m & 3)) & ((m >= 128) | ((m >> 2) <= (n >> 2)))
    s.bias[...] = jnp.where(ok, 0.0, -1e30)


def st_attend(s):
    scale = 1.0 / math.sqrt(HD)

    def body(c):
        at = rows(c, 128)
        for p in range(4):
            cs = slice(p * 128, (p + 1) * 128)
            qs = stack_heads(s.q[at, cs])
            kk = jnp.concatenate([s.k[at, cs], s.ks[at, cs]], axis=0)
            vv = jnp.concatenate([s.v[at, cs], s.vs[at, cs]], axis=0)
            b = s.bias[...]
            x = nt(qs, kk) * scale + jnp.concatenate([b, b], axis=0)
            m = jnp.max(x, axis=1, keepdims=True)
            e = jnp.exp(x - m)
            z = jnp.sum(e, axis=1, keepdims=True)
            pb = (e * (1.0 / z)).astype(BF)
            s.pr[p, c] = pb
            s.mix[at, cs] = pick_heads(nn(pb, vv)).astype(BF)
    loop(8, body)


def st_out(s, w, gain_ffn):
    def body(m):
        at = rows(m, 256)
        mid = s.tokp[at, :].astype(F32)
        for t in range(2):
            mid = mid + nt(s.mix[at, t * 256:(t + 1) * 256], w[t, :, OO:OO + HALF])
        s.mid[at, :] = mid
        xhat, _ = norm_rows(mid, None)
        s.nf[at, :] = (xhat * gain_ffn[...]).astype(BF)
    loop(4, body)


def gelu_pair(x):
    k0, k1 = math.sqrt(2.0 / math.pi), 0.044715
    x2 = x * x
    th = jnp.tanh(x * (k0 + (k0 * k1) * x2))
    half = 0.5 + 0.5 * th
    val = x * half
    der = half + (0.5 * x) * (1.0 - th * th) * (k0 + (3 * k0 * k1) * x2)
    return val, der


def st_ffn(s, w, g):
    for t in range(2):
        for u in range(2):
            ic = slice(IO + u * 512, IO + (u + 1) * 512)
            dc = slice(DO + u * 512, DO + (u + 1) * 512)
            first = t == 0 and u == 0

            def body(m, t=t, ic=ic, dc=dc, first=first):
                at = rows(m, 256)
                x = nn(s.nf[at, :], w[t, :, ic])
                gh = nn(s.cotp[at, :], w[t, :, dc])
                val, der = gelu_pair(x)
                hid = val.astype(BF)
                gp = (gh * der).astype(BF)
                s.hid[at, :] = hid
                s.gp[at, :] = gp
                add = nt(hid, w[t, :, dc])
                s.res[at, :] = (s.mid[at, :] if first else s.res[at, :]) + add
                add = nt(gp, w[t, :, ic])
                s.gnf[at, :] = add if first else s.gnf[at, :] + add
            loop(4, body)
            g[t, :, ic] = nn(s.nft[...], s.gp[...]).astype(BF)
            g[t, :, dc] = nn(s.cott[...], s.hid[...]).astype(BF)


def st_mid_back(s, w, g, gain_ffn):
    def body(m, acc):
        at = rows(m, 256)
        xhat, inv = norm_rows(s.mid[at, :], None)
        gnf = s.gnf[at, :]
        acc = acc + jnp.sum((gnf * xhat).reshape(32, 8, D), axis=0)
        gm = s.cotp[at, :].astype(F32) + norm_back(xhat, inv, gain_ffn[...], gnf)
        s.mid[at, :] = gm
        ga = gm.astype(BF)
        s.ga[at, :] = ga
        for t in range(2):
            s.gmix[at, t * 256:(t + 1) * 256] = nn(ga, w[t, :, OO:OO + HALF]).astype(BF)
        return acc
    acc = lax.fori_loop(0, 4, body, jnp.zeros((8, D), F32))
    s.gg[1:2, :] = jnp.sum(acc, axis=0, keepdims=True)
    transpose_into(s.gat, s.ga)
    for t in range(2):
        g[t, :, OO:OO + HALF] = nn(s.gat[...], s.mix[:, t * 256:(t + 1) * 256]).astype(BF)


def st_result(s, out, src):
    pm = order_matrix(True)

    def body(c):
        at = rows(c, 128)
        out[at, :] = nn(pm, src[at, :].astype(BF)).astype(BF)
    loop(8, body)


def st_attend_back(s):
    scale = 1.0 / math.sqrt(HD)

    def body(c):
        at = rows(c, 128)
        for p in range(4):
            cs = slice(p * 128, (p + 1) * 128)
            qs = stack_heads(s.q[at, cs])
            gs = stack_heads(s.gmix[at, cs])
            kk = jnp.concatenate([s.k[at, cs], s.ks[at, cs]], axis=0)
            vv = jnp.concatenate([s.v[at, cs], s.vs[at, cs]], axis=0)
            pb = s.pr[p, c]
            pf = pb.astype(F32)
            dp = nt(gs, vv)
            pd = pf * dp
            dl = jnp.sum(pd, axis=1, keepdims=True)
            ds = ((pd - pf * dl) * scale).astype(BF)
            s.dq[at, cs] = pick_heads(nn(ds, kk))
            dkk = tn(ds, qs)
            dvv = tn(pb, gs)
            s.dk[at, cs] = dkk[:128]
            s.dks[at, cs] = dkk[128:].astype(BF)
            s.dv[at, cs] = dvv[:128]
            s.dvs[at, cs] = dvv[128:].astype(BF)
    loop(8, body)


def st_sort_back(s):
    def body(rq, accs):
        new = []
        for p in range(4):
            cs = slice(p * 128, (p + 1) * 128)
            kv = jnp.concatenate([gather_chunk(s.k, rq, cs), gather_chunk(s.v, rq, cs)], axis=1)
            dkv = jnp.concatenate([gather_chunk(s.dks, rq, cs), gather_chunk(s.dvs, rq, cs)], axis=1)
            st = split_pair(dkv)
            new.append(accs[p] + nt(st, kv))
            lhs = jnp.concatenate([s.krt[2 * p], s.krt[2 * p + 1]], axis=1)
            out = nn(lhs, st)
            for i in range(8):
                at = pl.ds(pl.multiple_of(i * 128 + rq * 16, 16), 16)
                s.dk[at, cs] = s.dk[at, cs] + out[i * 16:(i + 1) * 16, 0:128]
                s.dv[at, cs] = s.dv[at, cs] + out[i * 16:(i + 1) * 16, 128:256]
        return tuple(new)
    accs = lax.fori_loop(0, 8, body, tuple(jnp.zeros((256, 128), F32) for _ in range(4)))
    a, b = iota((128, 128), 0), iota((128, 128), 1)
    same = ((a >> 2) & 3) == ((b >> 2) & 3)
    n = iota((128, NB), 0)
    e_mat = (((n >> 4) * 4 + (n & 3)) == iota((128, NB), 1)).astype(F32)
    for p in range(4):
        for e in range(2):
            x = jnp.where(same, accs[p][e * 128:(e + 1) * 128], 0.0)
            y = nn(x, e_mat, precision=HI)
            s.ds[(2 * p + e) * NB:(2 * p + e + 1) * NB, :] = tn(e_mat, y, precision=HI)


def st_sinkhorn_back(s):
    x = s.ds[...] * s.sk[2 * ITERS - 1]
    for it in reversed(range(ITERS)):
        y = x.reshape(8, NB, NB)
        pk = s.sk[2 * it + 1].reshape(8, NB, NB)
        x = (y - pk * jnp.sum(y, axis=1, keepdims=True)).reshape(8 * NB, NB)
        x = x - s.sk[2 * it] * jnp.sum(x, axis=1, keepdims=True)
    mask = jnp.concatenate([s.allow[...]] * 8, axis=0) > 0
    x = jnp.where(mask, x, 0.0) * (BLK / math.sqrt(HD) / BLK)
    for p in range(4):
        cs = slice(p * 128, (p + 1) * 128)
        x0, x1 = x[(2 * p) * NB:(2 * p + 1) * NB], x[(2 * p + 1) * NB:(2 * p + 2) * NB]
        ev = even_lanes((NB, 128))
        km, qm = s.km[:, cs], s.qm[:, cs]
        dqm = jnp.where(ev, nn(x0, km, precision=HI), nn(x1, km, precision=HI))
        dkm = jnp.where(ev, tn(x0, qm, precision=HI), tn(x1, qm, precision=HI))
        for c in range(8):
            for src, ref, dst in ((dqm, s.dq, s.dqb), (dkm, s.dk, s.dkb)):
                four = src[c * 4:(c + 1) * 4]
                eight = jnp.concatenate([four, four], axis=0)
                val = ref[c * 128:(c + 1) * 128, cs].reshape(16, 8, 128) + eight[None]
                dst[c * 128:(c + 1) * 128, cs] = val.reshape(128, 128).astype(BF)
    s.dvb[...] = s.dv[...].astype(BF)


def st_qkv_back(s, w, g, gain_attn):
    for t in range(2):
        cs = slice(t * 256, (t + 1) * 256)
        for off, ref in ((QO, s.dqb), (KO, s.dkb), (VO, s.dvb)):
            g[t, :, off:off + 256] = nn(s.nmt[...], ref[:, cs]).astype(BF)

    def body(m, acc):
        at = rows(m, 256)
        gn = jnp.zeros((256, D), F32)
        for t in range(2):
            cs = slice(t * 256, (t + 1) * 256)
            lhs = jnp.concatenate([s.dqb[at, cs], s.dkb[at, cs], s.dvb[at, cs]], axis=1)
            gn = gn + nt(lhs, w[t, :, 0:768])
        xhat, inv = norm_rows(s.tokp[at, :].astype(F32), None)
        acc = acc + jnp.sum((gn * xhat).reshape(32, 8, D), axis=0)
        s.mid[at, :] = s.mid[at, :] + norm_back(xhat, inv, gain_attn[...], gn)
        return acc
    acc = lax.fori_loop(0, 4, body, jnp.zeros((8, D), F32))
    s.gg[0:1, :] = jnp.sum(acc, axis=0, keepdims=True)


class Names:
    pass


def compute_all(s, tok, cot, gain_attn, gain_ffn, w, seg, result, gtok, g, stop=99):
    steps = [
        lambda: (st_tokens(s, tok, gain_attn), st_cot(s, cot)),
        lambda: (transpose_into(s.cott, s.cotp), transpose_into(s.nmt, s.nm), st_bias(s)),
        lambda: st_qkv(s, w),
        lambda: st_sinkhorn(s, seg),
        lambda: st_sort(s),
        lambda: st_attend(s),
        lambda: (st_out(s, w, gain_ffn), transpose_into(s.nft, s.nf)),
        lambda: st_ffn(s, w, g),
        lambda: st_result(s, result, s.res),
        lambda: st_mid_back(s, w, g, gain_ffn),
        lambda: st_attend_back(s),
        lambda: st_sort_back(s),
        lambda: st_sinkhorn_back(s),
        lambda: st_qkv_back(s, w, g, gain_attn),
        lambda: st_result(s, gtok, s.mid),
    ]
    for st in steps[:stop]:
        st()


def make_call(stop=99, interpret=False):
    names = list(SCRATCH)

    def kernel(tok, cot, ga, gf, w, seg, result, gtok, g, gg, *scr):
        s = Names()
        for n, r in zip(names, scr):
            setattr(s, n, r)
        compute_all(s, tok, cot, ga, gf, w, seg, result, gtok, g, stop)
        gg[...] = s.gg[...]
    vm = pl.BlockSpec(memory_space=pltpu.VMEM)
    return pl.pallas_call(
        kernel,
        out_shape=(jax.ShapeDtypeStruct((T, D), BF), jax.ShapeDtypeStruct((T, D), BF),
                   jax.ShapeDtypeStruct((2, D, COLS), BF), jax.ShapeDtypeStruct((8, D), F32)),
        in_specs=[vm] * 6, out_specs=(vm,) * 4,
        scratch_shapes=[pltpu.VMEM(*v) for v in SCRATCH.values()],
        compiler_params=pltpu.CompilerParams(vmem_limit_bytes=63 << 20),
        interpret=interpret,
    )


def gather_and_call(tokens, gain_attn, gain_ffn, w_query, w_key, w_value, w_out, w_in, w_down, segment_ids, cotangent):
    tp = lax.axis_index("tp")
    tok = lax.all_to_all(tokens, "tp", 0, 0, tiled=True).reshape(T, D)
    cot = lax.all_to_all(cotangent, "tp", 0, 0, tiled=True).reshape(T, D)
    own = jnp.concatenate([w_query, w_key, w_value, w_out.T, w_in, w_down.T], axis=1)
    half = lax.all_gather(own, "fsdp", axis=0, tiled=True)
    w = lax.all_gather(half, "tp", axis=0)
    seg = lax.dynamic_index_in_dim(segment_ids, tp, 0)
    res, gtok, g, gg = make_call()(tok, cot, gain_attn[None], gain_ffn[None], w, seg)
    res = lax.all_to_all(res.reshape(tokens.shape), "tp", 0, 0, tiled=True)
    gtok = lax.all_to_all(gtok.reshape(tokens.shape), "tp", 0, 0, tiled=True)
    gsum = lax.psum_scatter(g.astype(F32), "tp", scatter_dimension=0)
    gsum = lax.psum_scatter(gsum, "fsdp", scatter_dimension=0, tiled=True)
    gains = lax.psum_scatter(gg[:2], ("fsdp", "tp"), scatter_dimension=1, tiled=True)
    return (res, gtok, gains[0], gains[1], gsum[:, QO:KO], gsum[:, KO:VO], gsum[:, VO:OO],
            gsum[:, OO:IO].T, gsum[:, IO:DO], gsum[:, DO:].T)


def solution(mesh):
    return jax.shard_map(
        gather_and_call,
        mesh=mesh,
        in_specs=(P(None, ("fsdp", "tp"), None), P(), P(), P("fsdp", "tp"), P("fsdp", "tp"), P("fsdp", "tp"),
                  P("tp", "fsdp"), P("fsdp", "tp"), P("tp", "fsdp"), P(None, "fsdp"), P(None, ("fsdp", "tp"), None)),
        out_specs=(P(None, ("fsdp", "tp"), None), P(None, ("fsdp", "tp"), None), P(("fsdp", "tp")), P(("fsdp", "tp")),
                   P("fsdp", "tp"), P("fsdp", "tp"), P("fsdp", "tp"), P("tp", "fsdp"), P("fsdp", "tp"), P("tp", "fsdp")),
        check_vma=False,
    )
```

time: 1180 us -> 511 us (0.43)
  matrix products: 222 us -> 0 us
  waiting for transfers between devices: 574 us -> 372 us
  blocking collectives: 203 us -> 15 us
  Pallas kernels: 0 us -> 81 us
  other arithmetic: 87.4 us -> 8.96 us
  local copies, waits for them, and re-layouts: 57.9 us -> 14.7 us
    reduce_scatter x14 -> x2, waiting for transfers between devices: 430 us -> 167 us  [the longest x1 146 us: gather_and_call(): gsum = lax.psum_scatter(gsum, 'fsdp', scatter_dimension=0, tiled=True)]
    dot_general x78 -> x0, matrix products: 222 us -> none  [the longest x12 34.4 us: product(): return jnp.dot(left_arg, right_arg, preferred_element_type=jnp.float32)]
    all_gather x4 -> x0, blocking collectives: 161 us -> none  [the longest x1 43.8 us: per_device(): lax.all_gather(w_key, 'fsdp', axis=0, tiled=True)]
    unnamed x24 -> x6, waiting for transfers between devices: 2.91 us -> 128 us
    pallas_call x0 -> x1, Pallas kernels: none -> 81 us  [gather_and_call(): make_call()(tok, cot, gain_attn[None], gain_ffn[None], w, seg)]
    all_gather x10 -> x2, waiting for transfers between devices: 141 us -> 75.2 us  [the longest x1 70.9 us: gather_and_call(): half = lax.all_gather(own, 'fsdp', axis=0, tiled=True)]
    reduce_sum x78 -> x0, other arithmetic: 45 us -> none  [the longest x32 9.77 us: balanced_transport_kernel(): logits = logits - jax.nn.logsumexp(logits, axis=2, keepdims=True)]
    unnamed x1 -> x0, blocking collectives: 42 us -> none
  transfers between devices with their start and end apart: 24 -> 6, of which waited for: 17 -> 6; matrix products, arithmetic and copies ran while one was open for 12% -> 1% of each run, Pallas kernels for 0% -> 0%
where the time goes in v1:
time: 511 us; the launch traced here: 510 us
  waiting for transfers between devices  372 us (73%)
  Pallas kernels  81 us (16%)
  blocking collectives  15 us (3%)
  local copies, waits for them, and re-layouts  14.7 us (3%)
  between operations  13.9 us (3%)
  other arithmetic  8.96 us (2%)
    reduce_scatter x1, waiting for transfers between devices, gather_and_call(): gsum = lax.psum_scatter(gsum, 'fsdp', scatter_dimension=0, tiled=True)  146 us
    unnamed x6, waiting for transfers between devices  128 us
    pallas_call x1, Pallas kernels, gather_and_call(): make_call()(tok, cot, gain_attn[None], gain_ffn[None], w, seg)  81 us
    all_gather x1, waiting for transfers between devices, gather_and_call(): half = lax.all_gather(own, 'fsdp', axis=0, tiled=True)  70.9 us
    reduce_scatter x1, waiting for transfers between devices, gather_and_call(): gsum = lax.psum_scatter(g.astype(F32), 'tp', scatter_dimension=0)  20.9 us
  transfers between devices with their start and end apart: 6, of which 6 were waited for; matrix products, arithmetic and copies ran while one was open for 1% of the time, Pallas kernels for 0%

profile of v1, /device:TPU:0, one launch (start us, length us, event | category | flops | bytes accessed | tf_op | source)
XLA Modules:
  0.0 509.7 jit_solution(13613726182275970376)
XLA Ops:
  7.2 0.0 copy-start
  7.2 0.0 copy-start.1
  7.2 0.0 all-gather.4.cloned.1.call-start
  7.2 0.8 constant_dynamic-update-slice_fusion.3
  8.0 0.7 constant_dynamic-update-slice_fusion.2
  8.8 0.7 constant_dynamic-update-slice_fusion.1
  9.5 0.7 bitcast_dynamic-update-slice_fusion.1
  10.2 0.8 constant_dynamic-update-slice_fusion
  11.0 0.8 bitcast_dynamic-update-slice_fusion
  11.9 0.0 copy-start.4
  11.9 0.7 copy-done.4
  12.6 0.0 all-gather.4.cloned.1.call-update
  12.6 0.0 all-gather.6.cloned.1.call-start
  12.6 70.9 %all-gather.4.cloned.1.call-done = bf16[512,3072]{1,0:T(8,128)(2,1)} async-done(((bf16[32,3072]{1,0:T(8,128)(2,1)}), bf16[512,3072]{1,0:T(8,128)(2,1)}) %all-gather.4.cloned.1.call-update) | async-done | bytes 3145744 | tf_op jit(solution)/shard_map/all_gather | solution.py:452
  83.6 0.0 all-gather.6.cloned.1.call-update
  83.6 4.4 all-to-all-start
  88.1 0.0 reduce-scatter.6.cloned.1.call-start
  88.1 0.0 copy-done
  88.1 0.5 constant_dynamic-slice_fusion.seg
  88.6 1.6 all-to-all-done
  90.3 0.0 copy-done.1
  90.3 5.8 %all_to_all.20 = bf16[2,512,512]{2,1,0:T(8,128)(2,1)} all-to-all(bf16[2,512,512]{2,1,0:T(8,128)(2,1)S(1)} %copy-done.1), channel_id=1, replica_groups=mesh['fsdp'=16,'tp'=2] {'tp'}, dimensions={0} | all-to-all | bytes 2097152 | tf_op jit(solution)/shard_map/all_to_all | solution.py:450
  96.1 4.3 all-gather.6.cloned.1.call-done
  100.4 81.0 %shard_map.186 = (bf16[1024,512]{1,0:T(8,128)(2,1)}, bf16[1024,512]{1,0:T(8,128)(2,1)}, bf16[2,512,3072]{2,1,0:T(8,128)(2,1)}, f32[8,512]{1,0:T(8,128)}) custom-call(bf16[1024,512]{1,0:T(8,128)(2,1)} %bitcast.2.tok, bf16[1024,512]{1,0:T(8,128)(2,1)} %bitcast.22, f32[1,512]{1,0:T(1,128)} %bitcast.27, f32[1,512]{1,0:T(1,128)} %bitcast.28, ...), custom_call_target="tpu_custom_call" | custom-call | tf_op jit(solution)/shard_map/pallas_call | solution.py:455
  181.4 9.0 %convert_element_type.3 = f32[2,512,3072]{2,1,0:T(8,128)} convert(bf16[2,512,3072]{2,1,0:T(8,128)(2,1)} %get-tuple-element.17) | non-fusion elementwise | flops 3145728 | bytes 18874368 | tf_op jit(solution)/shard_map/convert_element_type | solution.py:458
  190.4 0.0 reduce-scatter.6.cloned.1.call-update
  190.4 0.0 copy-start.3
  190.4 0.0 copy-start.2
  190.4 0.0 reduce-scatter.10.cloned.1.call-start
  190.5 0.9 slice.27
  191.3 0.9 copy.21
  192.2 0.0 reduce-scatter.10.cloned.1.call-update
  192.2 0.0 reduce-scatter.8.cloned.1.call-start
  192.3 20.9 %reduce-scatter.6.cloned.1.call-done = f32[1,512,3072]{2,1,0:T(8,128)} async-done(((f32[2,512,3072]{2,1,0:T(8,128)}), f32[1,512,3072]{2,1,0:T(8,128)}) %reduce-scatter.6.cloned.1.call-update) | async-done | bytes 6291472 | tf_op jit(solution)/shard_map/reduce_scatter | solution.py:458
  213.2 0.0 reduce-scatter.8.cloned.1.call-update
  213.2 0.0 copy-done.3
  213.2 4.6 all_to_all.21
  217.8 0.0 copy-done.2
  217.8 4.6 all_to_all.22
  222.4 127.5 %reduce-scatter.10.cloned.1.call-done = f32[16,2]{1,0:T(8,128)} async-done(((f32[512,2]{1,0:T(8,128)}), f32[16,2]{1,0:T(8,128)}) %reduce-scatter.10.cloned.1.call-update) | async-done | bytes 144
  349.9 0.8 fusion
  350.7 0.6 copy.24
  351.3 0.6 copy.23
  351.9 146.2 %reduce-scatter.8.cloned.1.call-done = f32[32,3072]{1,0:T(8,128)} async-done(((f32[512,3072]{1,0:T(8,128)}), f32[32,3072]{1,0:T(8,128)}) %reduce-scatter.8.cloned.1.call-update) | async-done | bytes 393232 | tf_op jit(solution)/shard_map/reduce_scatter | solution.py:459
  498.1 1.5 slice_bitcast_fusion.1
  499.6 1.7 slice_bitcast_fusion
  501.2 1.0 copy.32
  502.2 1.0 copy.33
Async XLA Ops:
  7.2 80.9 %copy-start = (s32[2,32]{1,0:T(2,128)S(1)}, s32[2,32]{1,0:T(2,128)}, u32[]{:S(2)}) copy-start(s32[2,32]{1,0:T(2,128)} %param.20) | copy-start | bytes 772
  7.2 83.1 %copy-start.1 = (bf16[2,512,512]{2,1,0:T(8,128)(2,1)S(1)}, bf16[2,512,512]{2,1,0:T(8,128)(2,1)}, u32[]{:S(2)}) copy-start(bf16[2,512,512]{2,1,0:T(8,128)(2,1)} %param.21) | copy-start | bytes 3145732
  7.2 76.4 %all-gather.4.cloned.1.call-start = ((), (), s32[]{:S(2)}) async-start(), calls=%async_computation.7 | async-start | bytes 3342336 | tf_op jit(solution)/shard_map/all_gather | solution.py:452
  11.9 0.7 copy-start.4
  12.6 87.8 %all-gather.6.cloned.1.call-start = ((), (), s32[]{:S(2)}) async-start(), calls=%async_computation.10 | async-start | bytes 9437184 | tf_op jit(solution)/shard_map/all_gather | solution.py:453
  83.6 6.7 %all-to-all-start = ((bf16[2,512,512]{2,1,0:T(8,128)(2,1)}), bf16[2,512,512]{2,1,0:T(8,128)(2,1)}, u32[]{:S(2)}, u32[]{:S(2)}) async-start(bf16[2,512,512]{2,1,0:T(8,128)(2,1)} %param.11), calls=%async_computation | async-start | bytes 2097152 | tf_op jit(solution)/shard_map/all_to_all | solution.py:449
  88.1 125.1 %reduce-scatter.6.cloned.1.call-start = ((), (), s32[]{:S(2)}) async-start(), calls=%async_computation.8 | async-start | bytes 18874368 | tf_op jit(solution)/shard_map/reduce_scatter | solution.py:458
  190.4 22.8 %copy-start.3 = (bf16[1024,512]{1,0:T(8,128)(2,1)S(1)}, bf16[1024,512]{1,0:T(8,128)(2,1)}, u32[]{:S(2)}) copy-start(bf16[1024,512]{1,0:T(8,128)(2,1)} %get-tuple-element.15) | copy-start | bytes 3145732
  190.4 27.4 %copy-start.2 = (bf16[1024,512]{1,0:T(8,128)(2,1)S(1)}, bf16[1024,512]{1,0:T(8,128)(2,1)}, u32[]{:S(2)}) copy-start(bf16[1024,512]{1,0:T(8,128)(2,1)} %get-tuple-element.14) | copy-start | bytes 3145732
  190.4 159.5 %reduce-scatter.10.cloned.1.call-start = ((), (), s32[]{:S(2)}) async-start(), calls=%async_computation.11 | async-start | bytes 270336
  192.2 305.9 %reduce-scatter.8.cloned.1.call-start = ((), (), s32[]{:S(2)}) async-start(), calls=%async_computation.9 | async-start | bytes 6684672 | tf_op jit(solution)/shard_map/reduce_scatter | solution.py:459
Sparse Core Ops, SparseCore 0:
  12.7 70.8 all-gather.3
  85.1 15.2 all-gather.5
  190.5 22.6 reduce-scatter.5
  215.3 134.5 reduce-scatter.9
  355.8 142.2 reduce-scatter.7

commit v2 on v1

--- a/solution.py
+++ b/solution.py
@@ -10,7 +10,16 @@
 HD, BLK, ITERS, NB, D, FF, T = 64, 32, 8, 32, 512, 2048, 1024
 HALF = D // 2
 COLS = 3 * HALF + HALF + FF
-QO, KO, VO, OO, IO, DO = 0, 256, 512, 768, 1024, 2048
+QO, KO, VO, OO, FO = 0, 256, 512, 768, 1024
+UNITS = 512
+
+
+def in_cols(u):
+    return slice(FO + 2 * u * UNITS, FO + (2 * u + 1) * UNITS)
+
+
+def down_cols(u):
+    return slice(FO + (2 * u + 1) * UNITS, FO + (2 * u + 2) * UNITS)
 
 
 def nn(a, b, precision=None):
@@ -72,12 +81,11 @@
     qm=((NB, D), F32), km=((NB, D), F32), sk=((2 * ITERS, 8 * NB, NB), F32), allow=((NB, NB), F32),
     kr=((8, 128, 128), BF), krt=((8, 128, 128), BF), bias=((128, 256), F32),
     pr=((4, 8, 256, 256), BF), mix=((T, D), BF), mid=((T, D), F32), nf=((T, D), BF), nft=((D, T), BF),
-    hid=((T, 512), BF), gp=((T, 512), BF), res=((T, D), F32), gnf=((T, D), F32),
-    ga=((T, D), BF), gat=((D, T), BF), gmix=((T, D), BF),
-    dq=((T, D), F32), dk=((T, D), F32), dv=((T, D), F32), dks=((T, D), BF), dvs=((T, D), BF),
-    dqb=((T, D), BF), dkb=((T, D), BF), dvb=((T, D), BF), ds=((8 * NB, NB), F32),
+    hid=((T, UNITS), BF), gp=((T, UNITS), BF), res=((T, D), F32), gnf=((T, D), F32),
+    ga=((T, D), BF), gat=((D, T), BF), gmix=((T, D), BF), dv=((T, D), F32), ds=((8 * NB, NB), F32),
     gg=((8, D), F32),
 )
+SHARED = dict(dq="res", dk="gnf", dks="hid", dvs="gp", dqb="ga", dkb="nm", dvb="nf")
 
 
 def loop(n, body, unroll=1):
@@ -117,16 +125,23 @@
     return y[0:4] + y[4:8]
 
 
-def st_qkv(s, w):
+def st_values(s, w):
     def body(m):
         x = s.nm[rows(m, 256), :]
         for t in range(2):
-            out = nn(x, w[t, :, 0:768]).astype(BF)
+            s.v[rows(m, 256), t * 256:(t + 1) * 256] = nn(x, w[t, :, VO:VO + HALF]).astype(BF)
+    loop(4, body)
+
+
+def st_query_key(s, w):
+    def body(m):
+        x = s.nm[rows(m, 256), :]
+        for t in range(2):
+            out = nn(x, w[t, :, 0:512]).astype(BF)
             cs = slice(t * 256, (t + 1) * 256)
             qv, kv = out[:, 0:256], out[:, 256:512]
             s.q[rows(m, 256), cs] = qv
             s.k[rows(m, 256), cs] = kv
-            s.v[rows(m, 256), cs] = out[:, 512:768]
             for ref, val in ((s.qm, qv), (s.km, kv)):
                 val = val.astype(F32)
                 sums = jnp.concatenate([block_sums(val[:128]), block_sums(val[128:])], axis=0)
@@ -242,32 +257,37 @@
     return val, der
 
 
-def st_ffn(s, w, g):
-    for t in range(2):
-        for u in range(2):
-            ic = slice(IO + u * 512, IO + (u + 1) * 512)
-            dc = slice(DO + u * 512, DO + (u + 1) * 512)
-            first = t == 0 and u == 0
-
-            def body(m, t=t, ic=ic, dc=dc, first=first):
-                at = rows(m, 256)
-                x = nn(s.nf[at, :], w[t, :, ic])
-                gh = nn(s.cotp[at, :], w[t, :, dc])
-                val, der = gelu_pair(x)
-                hid = val.astype(BF)
-                gp = (gh * der).astype(BF)
-                s.hid[at, :] = hid
-                s.gp[at, :] = gp
-                add = nt(hid, w[t, :, dc])
-                s.res[at, :] = (s.mid[at, :] if first else s.res[at, :]) + add
-                add = nt(gp, w[t, :, ic])
-                s.gnf[at, :] = add if first else s.gnf[at, :] + add
-            loop(4, body)
-            g[t, :, ic] = nn(s.nft[...], s.gp[...]).astype(BF)
-            g[t, :, dc] = nn(s.cott[...], s.hid[...]).astype(BF)
-
-
-def st_mid_back(s, w, g, gain_ffn):
+def add_grads(g, other, t, own, cols, val):
+    if own:
+        val = val + other[:, :, :, cols].reshape(D, val.shape[1]).astype(F32)
+    g[t, :, :, :, cols] = val.astype(BF).reshape(4, 4, D // 16, val.shape[1])
+
+
+def st_ffn(s, w, t, u, first):
+    ic, dc = in_cols(u), down_cols(u)
+
+    def body(m):
+        at = rows(m, 256)
+        x = nn(s.nf[at, :], w[t, :, ic])
+        gh = nn(s.cotp[at, :], w[t, :, dc])
+        val, der = gelu_pair(x)
+        hid = val.astype(BF)
+        gp = (gh * der).astype(BF)
+        s.hid[at, :] = hid
+        s.gp[at, :] = gp
+        add = nt(hid, w[t, :, dc])
+        s.res[at, :] = (s.mid[at, :] if first else s.res[at, :]) + add
+        add = nt(gp, w[t, :, ic])
+        s.gnf[at, :] = add if first else s.gnf[at, :] + add
+    loop(4, body)
+
+
+def st_ffn_grads(s, g, other, t, u, own):
+    add_grads(g, other, t, own, in_cols(u), nn(s.nft[...], s.gp[...]))
+    add_grads(g, other, t, own, down_cols(u), nn(s.cott[...], s.hid[...]))
+
+
+def st_mid_back(s, w, gain_ffn):
     def body(m, acc):
         at = rows(m, 256)
         xhat, inv = norm_rows(s.mid[at, :], None)
@@ -283,8 +303,14 @@
     acc = lax.fori_loop(0, 4, body, jnp.zeros((8, D), F32))
     s.gg[1:2, :] = jnp.sum(acc, axis=0, keepdims=True)
     transpose_into(s.gat, s.ga)
-    for t in range(2):
-        g[t, :, OO:OO + HALF] = nn(s.gat[...], s.mix[:, t * 256:(t + 1) * 256]).astype(BF)
+
+
+def half_cols(t):
+    return pl.ds(pl.multiple_of(t * HALF, HALF), HALF)
+
+
+def st_out_grads(s, g, other, t, own):
+    add_grads(g, other, t, own, slice(OO, OO + HALF), nn(s.gat[...], s.mix[:, half_cols(t)]))
 
 
 def st_result(s, out, src):
@@ -296,7 +322,7 @@
     loop(8, body)
 
 
-def st_attend_back(s):
+def st_attend_back(s, lo, hi):
     scale = 1.0 / math.sqrt(HD)
 
     def body(c):
@@ -320,7 +346,7 @@
             s.dks[at, cs] = dkk[128:].astype(BF)
             s.dv[at, cs] = dvv[:128]
             s.dvs[at, cs] = dvv[128:].astype(BF)
-    loop(8, body)
+    lax.fori_loop(lo, hi, lambda i, z: (body(i), z)[1], 0)
 
 
 def st_sort_back(s):
@@ -376,12 +402,12 @@
     s.dvb[...] = s.dv[...].astype(BF)
 
 
-def st_qkv_back(s, w, g, gain_attn):
-    for t in range(2):
-        cs = slice(t * 256, (t + 1) * 256)
-        for off, ref in ((QO, s.dqb), (KO, s.dkb), (VO, s.dvb)):
-            g[t, :, off:off + 256] = nn(s.nmt[...], ref[:, cs]).astype(BF)
-
+def st_qkv_grads(s, g, other, t, own):
+    for off, ref in ((QO, s.dqb), (KO, s.dkb), (VO, s.dvb)):
+        add_grads(g, other, t, own, slice(off, off + HALF), nn(s.nmt[...], ref[:, half_cols(t)]))
+
+
+def st_qkv_back(s, w, gain_attn):
     def body(m, acc):
         at = rows(m, 256)
         gn = jnp.zeros((256, D), F32)
@@ -401,70 +427,372 @@
     pass
 
 
-def compute_all(s, tok, cot, gain_attn, gain_ffn, w, seg, result, gtok, g, stop=99):
-    steps = [
-        lambda: (st_tokens(s, tok, gain_attn), st_cot(s, cot)),
-        lambda: (transpose_into(s.cott, s.cotp), transpose_into(s.nmt, s.nm), st_bias(s)),
-        lambda: st_qkv(s, w),
-        lambda: st_sinkhorn(s, seg),
-        lambda: st_sort(s),
-        lambda: st_attend(s),
-        lambda: (st_out(s, w, gain_ffn), transpose_into(s.nft, s.nf)),
-        lambda: st_ffn(s, w, g),
-        lambda: st_result(s, result, s.res),
-        lambda: st_mid_back(s, w, g, gain_ffn),
-        lambda: st_attend_back(s),
-        lambda: st_sort_back(s),
-        lambda: st_sinkhorn_back(s),
-        lambda: st_qkv_back(s, w, g, gain_attn),
-        lambda: st_result(s, gtok, s.mid),
-    ]
-    for st in steps[:stop]:
-        st()
-
-
-def make_call(stop=99, interpret=False):
-    names = list(SCRATCH)
-
-    def kernel(tok, cot, ga, gf, w, seg, result, gtok, g, gg, *scr):
-        s = Names()
-        for n, r in zip(names, scr):
-            setattr(s, n, r)
-        compute_all(s, tok, cot, ga, gf, w, seg, result, gtok, g, stop)
-        gg[...] = s.gg[...]
+def stage_names(refs):
+    s = Names()
+    for n, r in zip(SCRATCH, refs):
+        setattr(s, n, r)
+    for n, o in SHARED.items():
+        setattr(s, n, getattr(s, o))
+    return s
+
+
+def layer_kernel(tok, cot, gain_attn, gain_ffn, w, seg, result, gtok, g, gg, *scr):
+    s = stage_names(scr)
+    st_tokens(s, tok, gain_attn)
+    st_cot(s, cot)
+    transpose_into(s.cott, s.cotp)
+    transpose_into(s.nmt, s.nm)
+    st_bias(s)
+    st_query_key(s, w)
+    st_sinkhorn(s, seg)
+    st_values(s, w)
+    st_sort(s)
+    st_attend(s)
+    st_out(s, w, gain_ffn)
+    transpose_into(s.nft, s.nf)
+    for t in range(2):
+        for u in range(2):
+            st_ffn(s, w, t, u, t + u == 0)
+            st_ffn_grads(s, g, None, t, u, False)
+    st_result(s, result, s.res)
+    st_mid_back(s, w, gain_ffn)
+    for t in range(2):
+        st_out_grads(s, g, None, t, False)
+    st_attend_back(s, 0, 8)
+    st_sort_back(s)
+    st_sinkhorn_back(s)
+    for t in range(2):
+        st_qkv_grads(s, g, None, t, False)
+    st_qkv_back(s, w, gain_attn)
+    st_result(s, gtok, s.mid)
+    gg[...] = s.gg[...]
+
+
+def layer_call():
     vm = pl.BlockSpec(memory_space=pltpu.VMEM)
     return pl.pallas_call(
-        kernel,
+        layer_kernel,
         out_shape=(jax.ShapeDtypeStruct((T, D), BF), jax.ShapeDtypeStruct((T, D), BF),
-                   jax.ShapeDtypeStruct((2, D, COLS), BF), jax.ShapeDtypeStruct((8, D), F32)),
+                   jax.ShapeDtypeStruct((2, 4, 4, D // 16, COLS), BF), jax.ShapeDtypeStruct((8, D), F32)),
         in_specs=[vm] * 6, out_specs=(vm,) * 4,
         scratch_shapes=[pltpu.VMEM(*v) for v in SCRATCH.values()],
-        compiler_params=pltpu.CompilerParams(vmem_limit_bytes=63 << 20),
-        interpret=interpret,
+        compiler_params=pltpu.CompilerParams(vmem_limit_bytes=60 << 20),
     )
 
 
-def gather_and_call(tokens, gain_attn, gain_ffn, w_query, w_key, w_value, w_out, w_in, w_down, segment_ids, cotangent):
+def split_cols(x):
+    ins = jnp.concatenate([x[:, in_cols(u)] for u in range(2)], axis=1)
+    downs = jnp.concatenate([x[:, down_cols(u)] for u in range(2)], axis=1)
+    return x[:, QO:KO], x[:, KO:VO], x[:, VO:OO], x[:, OO:FO], ins, downs
+
+
+def join_cols(q, k, v, o, i, d):
+    parts = [q, k, v, o]
+    for u in range(2):
+        parts += [i[:, u * UNITS:(u + 1) * UNITS], d[:, u * UNITS:(u + 1) * UNITS]]
+    return jnp.concatenate(parts, axis=1)
+
+
+def by_collectives(tokens, gain_attn, gain_ffn, w_query, w_key, w_value, w_out, w_in, w_down, segment_ids, cotangent):
     tp = lax.axis_index("tp")
     tok = lax.all_to_all(tokens, "tp", 0, 0, tiled=True).reshape(T, D)
     cot = lax.all_to_all(cotangent, "tp", 0, 0, tiled=True).reshape(T, D)
-    own = jnp.concatenate([w_query, w_key, w_value, w_out.T, w_in, w_down.T], axis=1)
+    own = join_cols(w_query, w_key, w_value, w_out.T, w_in, w_down.T)
     half = lax.all_gather(own, "fsdp", axis=0, tiled=True)
     w = lax.all_gather(half, "tp", axis=0)
     seg = lax.dynamic_index_in_dim(segment_ids, tp, 0)
-    res, gtok, g, gg = make_call()(tok, cot, gain_attn[None], gain_ffn[None], w, seg)
+    res, gtok, g, gg = layer_call()(tok, cot, gain_attn[None], gain_ffn[None], w, seg)
     res = lax.all_to_all(res.reshape(tokens.shape), "tp", 0, 0, tiled=True)
     gtok = lax.all_to_all(gtok.reshape(tokens.shape), "tp", 0, 0, tiled=True)
-    gsum = lax.psum_scatter(g.astype(F32), "tp", scatter_dimension=0)
+    gsum = lax.psum_scatter(g.reshape(2, D, COLS).astype(F32), "tp", scatter_dimension=0)
     gsum = lax.psum_scatter(gsum, "fsdp", scatter_dimension=0, tiled=True)
     gains = lax.psum_scatter(gg[:2], ("fsdp", "tp"), scatter_dimension=1, tiled=True)
-    return (res, gtok, gains[0], gains[1], gsum[:, QO:KO], gsum[:, KO:VO], gsum[:, VO:OO],
-            gsum[:, OO:IO].T, gsum[:, IO:DO], gsum[:, DO:].T)
+    q, k, v, o, i, d = split_cols(gsum)
+    return res, gtok, gains[0], gains[1], q, k, v, o.T, i, d.T
+
+
+PIECES = ((0, 512), (512, 1024), (1024, 2048), (2048, 3072))
+GPIECES = ((1024, 2048), (2048, 3072), (768, 1024), (0, 768))
+MESH = pl.DeviceIdType.MESH
+ROWS = D // 16
+
+EXCHANGE = dict(
+    w=((2, D, COLS), BF), g=((2, 4, 4, ROWS, COLS), BF), other=((4, 4, ROWS, COLS), BF),
+    rx=((3, 4, ROWS, COLS), BF), zs=((4, ROWS, COLS), BF), rz=((3, ROWS, COLS), BF),
+    tok=((T, D), BF), cot=((T, D), BF), gr=((7, 8, D), F32), gs=((3, 8, D), F32),
+)
+
+
+class Links:
+    def __init__(self, e, sems):
+        self.e = e
+        self.sems = sems
+        f, self.c = lax.axis_index("fsdp"), lax.axis_index("tp")
+        self.zi, self.xy = f // 4, f % 4
+        x, y = self.xy % 2, self.xy // 2
+        self.f = f
+        self.plane = [(1 - x) + 2 * y, x + 2 * (1 - y), (1 - x) + 2 * (1 - y)]
+        self.sent = []
+        self.copies = {}
+
+    def z_at(self, dz):
+        return (self.zi + dz) % 4
+
+    def z_from(self, dz):
+        return (self.zi + 4 - dz) % 4
+
+    def everyone(self):
+        return ([(self.z_at(d) * 4 + self.xy, self.c) for d in (1, 2, 3)]
+                + [(self.zi * 4 + k, self.c) for k in self.plane] + [(self.f, 1 - self.c)])
+
+    def meet(self):
+        bar = pltpu.get_barrier_semaphore()
+        for dev in self.everyone():
+            pl.semaphore_signal(bar, inc=1, device_id=dev, device_id_type=MESH)
+        pl.semaphore_wait(bar, 7)
+
+    def send(self, key, src, dst, sem, dev):
+        send_sem, recv_sem = self.sems
+        copy = pltpu.make_async_remote_copy(src_ref=src, dst_ref=dst, send_sem=send_sem.at[sem], recv_sem=recv_sem.at[sem],
+                                            device_id=dev, device_id_type=MESH)
+        copy.start()
+        self.sent.append(copy)
+        self.copies[key] = copy
+
+    def arrived(self, key):
+        self.copies[key].wait_recv()
+
+    def finish(self):
+        for copy in self.sent:
+            copy.wait_send()
+
+    def own_rows(self, piece):
+        cols = slice(*PIECES[piece])
+        w = self.e.w
+        at = w.at[self.c, pl.ds(pl.multiple_of(self.f * ROWS, ROWS), ROWS), cols]
+        for d in (1, 2, 3):
+            self.send(("z", piece, d), at, at, 19 * piece + d - 1, (self.z_at(d) * 4 + self.xy, self.c))
+        for n, k in enumerate(self.plane):
+            self.send(("p", piece, 0, n), at, at, 19 * piece + 3 + n, (self.zi * 4 + k, self.c))
+
+    def pass_plane(self, piece):
+        cols = slice(*PIECES[piece])
+        for d in (1, 2, 3):
+            self.arrived(("z", piece, d))
+            row = (self.z_from(d) * 4 + self.xy) * ROWS
+            at = self.e.w.at[self.c, pl.ds(pl.multiple_of(row, ROWS), ROWS), cols]
+            for n, k in enumerate(self.plane):
+                self.send(("p", piece, d, n), at, at, 19 * piece + 3 + 3 * d + n, (self.zi * 4 + k, self.c))
+
+    def pass_pair(self, piece):
+        cols = slice(*PIECES[piece])
+        for d in range(4):
+            for n in range(3):
+                self.arrived(("p", piece, d, n))
+            row = self.z_from(d) * 4 * ROWS
+            at = self.e.w.at[self.c, pl.ds(pl.multiple_of(row, 4 * ROWS), 4 * ROWS), cols]
+            self.send(("t", piece, d), at, at, 19 * piece + 15 + d, (self.f, 1 - self.c))
+
+    def gathered(self, piece):
+        for d in range(4):
+            self.arrived(("t", piece, d))
+
+    def grads_pair(self, piece):
+        cols = slice(*GPIECES[piece])
+        self.send(("gt", piece), self.e.g.at[1 - self.c, :, :, :, cols], self.e.other.at[:, :, :, cols], 76 + 7 * piece,
+                  (self.f, 1 - self.c))
+
+    def grads_pair_in(self, piece):
+        self.arrived(("gt", piece))
+
+    def grads_plane(self, piece):
+        cols = slice(*GPIECES[piece])
+        for n, k in enumerate(self.plane):
+            self.send(("gp", piece, n), self.e.g.at[self.c, :, k, :, cols], self.e.rx.at[n, :, :, cols], 77 + 7 * piece + n,
+                      (self.zi * 4 + k, self.c))
+
+    def grads_line(self, piece, out):
+        e = self.e
+        cols = slice(*GPIECES[piece])
+        for n in range(3):
+            self.arrived(("gp", piece, n))
+        for d in (1, 2, 3):
+            z = self.z_at(d)
+            total = e.g[self.c, z, self.xy, :, cols].astype(F32)
+            for n in range(3):
+                total = total + e.rx[n, z, :, cols].astype(F32)
+            e.zs[d, :, cols] = total.astype(BF)
+            self.send(("gz", piece, d), e.zs.at[d, :, cols], e.rz.at[d - 1, :, cols], 79 + 7 * piece + d, (z * 4 + self.xy, self.c))
+        total = e.g[self.c, self.zi, self.xy, :, cols].astype(F32)
+        for n in range(3):
+            total = total + e.rx[n, self.zi, :, cols].astype(F32)
+        out[:, cols] = total
+
+    def grads_in(self, piece, out):
+        cols = slice(*GPIECES[piece])
+        for d in (1, 2, 3):
+            self.arrived(("gz", piece, d))
+        total = out[:, cols]
+        for d in range(3):
+            total = total + self.e.rz[d, :, cols].astype(F32)
+        out[:, cols] = total
+
+    def gains_sum(self, step):
+        e = self.e
+        if step == 0:
+            self.send(("n", 0), e.gs.at[0], e.gr.at[0], 104, (self.f, 1 - self.c))
+        if step == 1:
+            self.arrived(("n", 0))
+            e.gs[1] = e.gs[0] + e.gr[0]
+            for n, k in enumerate(self.plane):
+                self.send(("n", 1 + n), e.gs.at[1], e.gr.at[1 + n], 105 + n, (self.zi * 4 + k, self.c))
+        if step == 2:
+            for n in range(3):
+                self.arrived(("n", 1 + n))
+            e.gs[2] = e.gs[1] + e.gr[1] + e.gr[2] + e.gr[3]
+            for d in (1, 2, 3):
+                self.send(("n", 3 + d), e.gs.at[2], e.gr.at[3 + d], 107 + d, (self.z_at(d) * 4 + self.xy, self.c))
+        if step == 3:
+            for d in (1, 2, 3):
+                self.arrived(("n", 3 + d))
+            return e.gs[2] + e.gr[4] + e.gr[5] + e.gr[6]
+
+
+NSEM = 116
+
+
+def step_kernel(tokens, cotangent, gain_attn, gain_ffn, wq, wk, wv, wo, wi, wd, seg, result, gtok, gains, gout, *scr):
+    ns, ne = len(SCRATCH), len(EXCHANGE)
+    s = stage_names(scr[:ns])
+    e = Names()
+    for n, r in zip(EXCHANGE, scr[ns:ns + ne]):
+        setattr(e, n, r)
+    send_sem, recv_sem, local = scr[ns + ne:]
+    link = Links(e, (send_sem, recv_sem))
+    c, f, w, g = link.c, link.f, e.w, e.g
+    half = T // 2
+    mine = pl.ds(pl.multiple_of(c * half, half), half)
+    theirs = pl.ds(pl.multiple_of((1 - c) * half, half), half)
+    pair = (f, 1 - c)
+
+    loads = [pltpu.make_async_copy(tokens.at[c], e.tok.at[mine, :], local.at[0]),
+             pltpu.make_async_copy(cotangent.at[c], e.cot.at[mine, :], local.at[1])]
+    for cp in loads:
+        cp.start()
+    own = join_cols(wq[...], wk[...], wv[...], jnp.transpose(wo[...], (1, 0)), wi[...], jnp.transpose(wd[...], (1, 0)))
+    w[c, pl.ds(pl.multiple_of(f * ROWS, ROWS), ROWS), :] = own
+    link.meet()
+    link.own_rows(0)
+    link.send("tok", tokens.at[1 - c], e.tok.at[mine, :], 111, pair)
+    link.send("cot", cotangent.at[1 - c], e.cot.at[mine, :], 112, pair)
+    loads[0].wait()
+    link.arrived("tok")
+    st_tokens(s, e.tok, gain_attn)
+    link.pass_plane(0)
+    link.own_rows(1)
+    loads[1].wait()
+    link.arrived("cot")
+    st_cot(s, e.cot)
+    transpose_into(s.cott, s.cotp)
+    transpose_into(s.nmt, s.nm)
+    st_bias(s)
+    link.pass_pair(0)
+    link.pass_plane(1)
+    link.own_rows(2)
+    link.gathered(0)
+    st_query_key(s, w)
+    link.pass_pair(1)
+    link.pass_plane(2)
+    link.own_rows(3)
+    st_sinkhorn(s, seg.at[pl.ds(c, 1), :])
+    link.gathered(1)
+    st_values(s, w)
+    st_sort(s)
+    link.pass_pair(2)
+    link.pass_plane(3)
+    st_attend(s)
+    st_out(s, w, gain_ffn)
+    transpose_into(s.nft, s.nf)
+    link.pass_pair(3)
+    link.gathered(2)
+    for u in range(2):
+        if u == 1:
+            link.gathered(3)
+        st_ffn(s, w, 1 - c, u, u == 0)
+        st_ffn_grads(s, g, None, 1 - c, u, False)
+        link.grads_pair(u)
+        st_ffn(s, w, c, u, False)
+        link.grads_pair_in(u)
+        st_ffn_grads(s, g, e.other, c, u, True)
+        link.grads_plane(u)
+    st_result(s, e.tok, s.res)
+    stores = [pltpu.make_async_copy(e.tok.at[mine, :], result.at[c], local.at[2])]
+    stores[0].start()
+    link.send("res", e.tok.at[theirs, :], result.at[c], 113, pair)
+    st_mid_back(s, w, gain_ffn)
+    st_out_grads(s, g, None, 1 - c, False)
+    link.grads_pair(2)
+    link.grads_line(0, gout)
+    link.grads_pair_in(2)
+    st_out_grads(s, g, e.other, c, True)
+    link.grads_plane(2)
+    st_attend_back(s, 0, 4)
+    link.grads_in(0, gout)
+    link.grads_line(1, gout)
+    st_attend_back(s, 4, 8)
+    link.grads_in(1, gout)
+    link.grads_line(2, gout)
+    st_sort_back(s)
+    st_sinkhorn_back(s)
+    st_qkv_grads(s, g, None, 1 - c, False)
+    link.grads_pair(3)
+    link.grads_in(2, gout)
+    st_qkv_back(s, w, gain_attn)
+    e.gs[0] = s.gg[...]
+    link.gains_sum(0)
+    link.grads_pair_in(3)
+    st_qkv_grads(s, g, e.other, c, True)
+    link.grads_plane(3)
+    link.gains_sum(1)
+    st_result(s, e.cot, s.mid)
+    stores.append(pltpu.make_async_copy(e.cot.at[mine, :], gtok.at[c], local.at[3]))
+    stores[1].start()
+    link.send("gtok", e.cot.at[theirs, :], gtok.at[c], 114, pair)
+    link.gains_sum(2)
+    link.grads_line(3, gout)
+    total = link.gains_sum(3)
+    width = gains.shape[1]
+    pick = (iota((D, width), 0) == iota((D, width), 1) + (2 * f + c) * width).astype(F32)
+    gains[...] = nn(total, pick, precision=HI)
+    link.grads_in(3, gout)
+    link.arrived("res")
+    link.arrived("gtok")
+    for cp in stores:
+        cp.wait()
+    link.finish()
+
+
+def by_kernel(tokens, gain_attn, gain_ffn, w_query, w_key, w_value, w_out, w_in, w_down, segment_ids, cotangent):
+    vm, hbm = pl.BlockSpec(memory_space=pltpu.VMEM), pl.BlockSpec(memory_space=pl.ANY)
+    width = D // 32
+    shapes = list(SCRATCH.values()) + list(EXCHANGE.values())
+    res, gtok, gains, gout = pl.pallas_call(
+        step_kernel,
+        out_shape=(jax.ShapeDtypeStruct(tokens.shape, BF), jax.ShapeDtypeStruct(tokens.shape, BF),
+                   jax.ShapeDtypeStruct((8, width), F32), jax.ShapeDtypeStruct((ROWS, COLS), F32)),
+        in_specs=[hbm] * 2 + [vm] * 9, out_specs=(hbm, hbm, vm, vm),
+        scratch_shapes=[pltpu.VMEM(*v) for v in shapes] + [
+            pltpu.SemaphoreType.DMA((NSEM,)), pltpu.SemaphoreType.DMA((NSEM,)), pltpu.SemaphoreType.DMA((4,))],
+        compiler_params=pltpu.CompilerParams(collective_id=0, has_side_effects=True, vmem_limit_bytes=63 << 20),
+    )(tokens, cotangent, gain_attn[None], gain_ffn[None], w_query, w_key, w_value, w_out, w_in, w_down, segment_ids)
+    q, k, v, o, i, d = split_cols(gout)
+    return res, gtok, gains[0], gains[1], q, k, v, o.T, i, d.T
 
 
 def solution(mesh):
+    body = by_kernel if mesh.shape["fsdp"] == 16 else by_collectives
     return jax.shard_map(
-        gather_and_call,
+        body,
         mesh=mesh,
         in_specs=(P(None, ("fsdp", "tp"), None), P(), P(), P("fsdp", "tp"), P("fsdp", "tp"), P("fsdp", "tp"),
                   P("tp", "fsdp"), P("fsdp", "tp"), P("tp", "fsdp"), P(None, "fsdp"), P(None, ("fsdp", "tp"), None)),

time: 511 us -> 131 us (0.26)
  waiting for transfers between devices: 372 us -> 0 us
  Pallas kernels: 81 us -> 120 us
  blocking collectives: 15 us -> 0 us
  between operations: 13.9 us -> 0.68 us
  other arithmetic: 8.96 us -> 0.72 us
  local copies, waits for them, and re-layouts: 14.7 us -> 8.77 us
    reduce_scatter x2 -> x0, waiting for transfers between devices: 167 us -> none  [the longest x1 146 us: gather_and_call(): gsum = lax.psum_scatter(gsum, 'fsdp', scatter_dimension=0, tiled=True)]
    unnamed x6 -> x0, waiting for transfers between devices: 128 us -> none
    all_gather x2 -> x0, waiting for transfers between devices: 75.2 us -> none  [the longest x1 70.9 us: gather_and_call(): half = lax.all_gather(own, 'fsdp', axis=0, tiled=True)]
    pallas_call x1, Pallas kernels: 81 us -> 120 us  [by_kernel(): pl.pallas_call(step_kernel, out_shape=(jax.ShapeDtypeStruct(tokens.shape,...]
    all_to_all x3 -> x0, blocking collectives: 15 us -> none  [the longest x1 5.82 us: gather_and_call(): cot = lax.all_to_all(cotangent, 'tp', 0, 0, tiled=True).reshape(T, D)]
    convert_element_type x1 -> x0, other arithmetic: 8.96 us -> none  [gather_and_call(): gsum = lax.psum_scatter(g.astype(F32), 'tp', scatter_dimension=0)]
  transfers between devices with their start and end apart: 6 -> 0, of which waited for: 6 -> 0; matrix products, arithmetic and copies ran while one was open for 1% -> 0% of each run, Pallas kernels for 0% -> 0%
where the time goes in v2:
time: 131 us; the launch traced here: 130 us
  Pallas kernels  120 us (92%)
  local copies, waits for them, and re-layouts  8.77 us (7%)
    pallas_call x1, Pallas kernels, by_kernel(): pl.pallas_call(step_kernel, out_shape=(jax.ShapeDtypeStruct(tokens.shape,...  120 us
    unnamed x10, local copies, waits for them, and re-layouts  5 us

profile of v2, /device:TPU:0, one launch (start us, length us, event | category | flops | bytes accessed | tf_op | source)
XLA Modules:
  0.0 130.4 jit_solution(18060675462573652336)
XLA Ops:
  0.6 0.0 copy-start.2
  0.7 1.7 %copy.22.wd = bf16[1024,32]{1,0:T(8,128)(2,1)} copy(bf16[1024,32]{0,1:T(8,128)(2,1)} %param.19) | data formatting | bytes 131072 | tf_op args[8]
  2.3 0.0 copy-done.2
  2.3 0.7 copy.21.wo
  3.1 120.2 %shard_map.186 = (bf16[2,512,512]{2,1,0:T(8,128)(2,1)}, bf16[2,512,512]{2,1,0:T(8,128)(2,1)}, f32[8,16]{1,0:T(8,128)}, f32[32,3072]{1,0:T(8,128)}) custom-call(bf16[2,512,512]{2,1,0:T(8,128)(2,1)} %tokens.1, bf16[2,512,512]{2,1,0:T(8,128)(2,1)} %cotangent.1, f32[1,512]{1,0:T(1,128)} %bitcast.10, f32[1,512]{1,0:T(1,128)} %bitcast.11, bf16[32,256]{1,0:T(8,128)(2,1)} %wq.1, ...), custom_call_target="tpu_custom_call" | custom-call | tf_op jit(solution)/shard_map/pallas_call | solution.py:779
  123.3 0.0 copy-start.1
  123.3 1.0 fusion
  124.3 0.7 pad_maximum_fusion
  125.1 1.5 %slice_bitcast_fusion = (f32[256,32]{0,1:T(8,128)}, f32[32,256]{1,0:T(8,128)}, f32[32,256]{1,0:T(8,128)}, f32[32,256]{1,0:T(8,128)}) fusion(f32[32,3072]{1,0:T(8,128)} %get-tuple-element.17), kind=kLoop, calls=%fused_computation.2 | loop fusion | bytes 262144 | tf_op jit(solution)/shard_map/transpose | solution.py:789
  126.5 1.3 slice_bitcast_fusion.1
  127.8 0.0 copy-done.1
  127.8 0.0 copy-start
  127.8 1.0 copy.25
  128.8 0.6 copy-done
  129.4 1.0 copy.26
Async XLA Ops:
  0.6 1.7 %copy-start.2 = (bf16[256,32]{0,1:T(8,128)(2,1)S(1)}, bf16[256,32]{0,1:T(8,128)(2,1)}, u32[]{:S(2)}) copy-start(bf16[256,32]{0,1:T(8,128)(2,1)} %param.17) | copy-start | bytes 49156
  123.3 4.5 %copy-start.1 = (bf16[2,512,512]{2,1,0:T(8,128)(2,1)S(1)}, bf16[2,512,512]{2,1,0:T(8,128)(2,1)}, u32[]{:S(2)}) copy-start(bf16[2,512,512]{2,1,0:T(8,128)(2,1)} %get-tuple-element.40) | copy-start | bytes 3145732
  127.8 1.6 %copy-start = (bf16[2,512,512]{2,1,0:T(8,128)(2,1)S(1)}, bf16[2,512,512]{2,1,0:T(8,128)(2,1)}, u32[]{:S(2)}) copy-start(bf16[2,512,512]{2,1,0:T(8,128)(2,1)} %get-tuple-element.41) | copy-start | bytes 3145732
